TPU v7x, 512 devices: a whole 4x8x8 slice. The times are simulated.
512 devices in a mesh: head: 8 (over x, core), pos: 64 (over z, y).
Axes of the slice: x: 4, y: 8, z: 8, core: 2. Of those that a mesh axis runs over, the one named last changes fastest.
Arguments:
- ref_queries: bfloat16 [8, 512, 128], P('head', 'pos'), may hold values from -128 to 128
- query_pos: int32 [8, 512], P('head', 'pos'), may hold values from 0 to 32767, as said below
- cache_keys: bfloat16 [8, 32768, 128], P('head', 'pos'), may hold values from -8 to 8
- cache_values: bfloat16 [8, 32768, 128], P('head', 'pos'), may hold values from -24 to 24
- slot_index: int32 [8, 512], P('head'), may hold values from 0 to 32767, as said below
Outputs:
- ref_output: bfloat16 [8, 512, 128], P('head', 'pos')
- compact_values: float32 [8, 512, 128], P('head')
Inputs may be any that keep to these rules, and one draw needn't show every extreme that they name: `query_pos`: along each head's rows the positions never fall; the first is 0 and the last 32767. `slot_index`: within a head the slots hold distinct positions; slot 0 holds position 0 and slot 1 holds position 32767.
All inputs are finite; a program needn't handle non-finite values.
Results may differ from a plain program's by a relative error of at most 0.0042.
Values may be sent and summed in bfloat16 or wider, within the bound.
A program may use at most 64 MiB of HBM per device.

v0:
```python
import math

import jax
import jax.numpy as jnp
from jax import lax
from jax.sharding import PartitionSpec as P

RIDGE = 1.0
NEG_FILL = -1e30


def block_partials(query_block, qpos_block, key_block, value_block, key_base, inv_root):
    scores = jnp.dot(query_block, key_block.T, preferred_element_type=jnp.float32) * inv_root
    key_pos = key_base + jnp.arange(key_block.shape[0], dtype=jnp.int32)
    allowed = key_pos[None, :] <= qpos_block[:, None]
    masked = jnp.where(allowed, scores, NEG_FILL)
    block_top = jnp.max(masked, axis=1)
    weights = jnp.where(allowed, jnp.exp(masked - block_top[:, None]), 0.0)
    weight_sum = jnp.sum(weights, axis=1)
    numerators = jnp.dot(
        weights.astype(jnp.bfloat16), value_block, preferred_element_type=jnp.float32
    )
    return (block_top, weight_sum, numerators)


def local_partials(queries_all, qpos_all, key_block, value_block, key_base, inv_root):
    row_total = queries_all.shape[0]
    block_rows = min(512, row_total)
    block_count = row_total // block_rows

    def one_block(pieces):
        return block_partials(pieces[0], pieces[1], key_block, value_block, key_base, inv_root)

    maxima, totals, numerators = lax.map(
        one_block,
        (
            queries_all.reshape(block_count, block_rows, -1),
            qpos_all.reshape(block_count, block_rows),
        ),
    )
    return (maxima.reshape(row_total), totals.reshape(row_total), numerators.reshape(row_total, -1))


def feature_terms(query_rows, qpos_rows, out_rows, compact, slot_pos, inv_root):
    logits = jnp.dot(query_rows, compact.T, preferred_element_type=jnp.float32) * inv_root
    allowed = slot_pos[None, :] <= qpos_rows[:, None]
    masked = jnp.where(allowed, logits, NEG_FILL)
    row_top = jnp.max(masked, axis=1, keepdims=True)
    raw_weights = jnp.where(allowed, jnp.exp(masked - row_top), 0.0)
    features = (raw_weights / jnp.sum(raw_weights, axis=1, keepdims=True)).astype(jnp.bfloat16)
    gram_sum = jnp.dot(features.T, features, preferred_element_type=jnp.float32)
    cross_sum = jnp.dot(features.T, out_rows, preferred_element_type=jnp.float32)
    return (gram_sum, cross_sum)


def feature_sums(query_rows, qpos_rows, out_rows, compact, slot_pos, inv_root):
    row_total = query_rows.shape[0]
    block_rows = min(512, row_total)
    block_count = row_total // block_rows
    slot_count = compact.shape[0]

    def add_block(running, pieces):
        gram_sum, cross_sum = feature_terms(
            pieces[0], pieces[1], pieces[2], compact, slot_pos, inv_root
        )
        return ((running[0] + gram_sum, running[1] + cross_sum), None)

    start = (
        jnp.zeros((slot_count, slot_count), jnp.float32),
        jnp.zeros((slot_count, out_rows.shape[1]), jnp.float32),
    )
    blocks = (
        query_rows.reshape(block_count, block_rows, -1),
        qpos_rows.reshape(block_count, block_rows),
        out_rows.reshape(block_count, block_rows, -1),
    )
    (gram_sum, cross_sum), _ = lax.scan(add_block, start, blocks)
    return (gram_sum, cross_sum)


def ridge_solve(gram_sum, cross_sum):
    identity = jnp.eye(gram_sum.shape[0], dtype=jnp.float32)
    factor_low = jnp.linalg.cholesky(gram_sum + RIDGE * identity)
    return jax.scipy.linalg.cho_solve((factor_low, True), cross_sum)


def shards(ref_queries, query_pos, cache_keys, cache_values, slot_index):
    inv_root = 1.0 / math.sqrt(cache_keys.shape[2])
    key_block = cache_keys[0]
    value_block = cache_values[0]
    block_width = key_block.shape[0]
    key_base = lax.axis_index("pos") * block_width
    slots = slot_index[0]
    local_slot = slots - key_base
    present = (local_slot >= 0) & (local_slot < block_width)
    picked = jnp.where(
        present[:, None],
        key_block[jnp.clip(local_slot, 0, block_width - 1)].astype(jnp.float32),
        0.0,
    )
    compact = lax.psum(picked, "pos").astype(jnp.bfloat16)
    queries_all, qpos_all = (
        lax.all_gather(ref_queries, "pos", axis=1, tiled=True),
        lax.all_gather(query_pos, "pos", axis=1, tiled=True),
    )
    maxima, totals, numerators = local_partials(
        queries_all[0], qpos_all[0], key_block, value_block, key_base, inv_root
    )
    row_top = lax.pmax(maxima, "pos")
    scales = jnp.exp(maxima - row_top)
    numer_here, total_here = (
        lax.psum_scatter(numerators * scales[:, None], "pos", scatter_dimension=0, tiled=True),
        lax.psum_scatter(totals * scales, "pos", scatter_dimension=0, tiled=True),
    )
    attended = (numer_here / total_here[:, None]).astype(jnp.bfloat16)
    gram_part, cross_part = feature_sums(
        ref_queries[0], query_pos[0], attended, compact, slots, inv_root
    )
    gram_sum, cross_sum = lax.psum((gram_part, cross_part), "pos")
    fitted = ridge_solve(gram_sum, cross_sum)
    return (attended[None], fitted[None])


def solution(mesh):
    in_specs = (
        P("head", "pos", None),
        P("head", "pos"),
        P("head", "pos", None),
        P("head", "pos", None),
        P("head", None),
    )
    out_specs = (P("head", "pos", None), P("head", None, None))
    return jax.shard_map(shards, mesh=mesh, in_specs=in_specs, out_specs=out_specs, check_vma=False)
```

profile of v0, /device:TPU:6, one launch (start us, length us, event | category | flops | bytes accessed | tf_op | source)
XLA Modules:
  0.0 813.5 jit_solution(5674048074913140118)
XLA Ops:
  7.9 56.5 %all_gather.7 = bf16[1,512,128]{2,1,0:T(8,128)(2,1)S(1)} all-gather(bf16[1,8,128]{2,1,0:T(8,128)(2,1)S(1)} %copy-done.5), channel_id=1, replica_groups=mesh['head'=8,'pos'=64] {'pos'}, dimensions={1}, use_global_device_ids=true | all-gather | bytes 133120 | tf_op jit(solution)/shard_map/all_gather | solution.py:103
  67.1 22.4 %all-reduce.1 = s32[512]{0:T(512)S(1)} all-reduce(s32[512]{0:T(512)S(1)} %bitcast_dynamic-update-slice_fusion.1), channel_id=1, replica_groups=mesh['head'=8,'pos'=64] {'pos'}, use_global_device_ids=true, to_apply=%add.1 | all-reduce | flops 512 | bytes 4096
  89.9 140.0 %pmax.7 = f32[512]{0:T(512)S(1)} all-reduce(f32[512]{0:T(512)S(1)} %get-tuple-element.89), channel_id=1, replica_groups=mesh['head'=8,'pos'=64] {'pos'}, use_global_device_ids=true, to_apply=%region_1.2 | all-reduce | flops 512 | bytes 4096 | tf_op jit(solution)/shard_map/pmax | solution.py:109
  230.8 1.1 convolution_multiply_fusion.1
  232.6 1.3 gather_fusion
  234.1 276.9 %all-reduce.13 = (f32[512]{0:T(512)S(1)}, bf16[512,128]{1,0:T(8,128)(2,1)S(1)}) all-reduce(f32[512]{0:T(512)S(1)} %get-tuple-element.73, f32[512,128]{1,0:T(8,128)S(1)} %convert_select_fusion), channel_id=3, replica_groups=mesh['head'=8,'pos'=64] {'pos'}, use_global_device_ids=true, to_apply=%region_4.5.clone | all-reduce | flops 66048 | bytes 397312
  512.2 1.4 fusion.66
  513.6 1.7 fusion.65
  515.4 1.3 fusion.84
  516.7 151.9 %all-reduce.12.cloned.1.call-done = (f32[512,512]{0,1:T(8,128)}, f32[512,128]{1,0:T(8,128)}) async-done(((f32[512,512]{0,1:T(8,128)}, f32[512,128]{1,0:T(8,128)}), (f32[512,512]{0,1:T(8,128)}, f32[512,128]{1,0:T(8,128)})) %all-reduce.12.cloned.1.call-update) | async-done | bytes 1310736 | tf_op jit(solution)/shard_map/psum | solution.py:119
  668.6 1.3 convert_add_fusion
  671.4 11.7 %cholesky.103 = f32[128,128]{1,0:T(8,128)S(1)} custom-call(f32[128,128]{1,0:T(8,128)S(1)} %cholesky.263), custom_call_target="Cholesky" | custom-call | tf_op jit(solution)/shard_map/jit(cholesky)/cholesky | solution.py:83
  683.3 9.8 %custom-call.34 = f32[1,128,128]{1,2,0:T(8,128)S(1)} custom-call(f32[1,128,128]{2,1,0:T(8,128)S(1)} %get-tuple-element.86), custom_call_target="InvertDiagBlocksLowerTriangular" | custom-call | tf_op jit(solution)/shard_map/jit(cholesky)/cholesky | solution.py:83
  693.8 11.7 %cholesky.215 = f32[128,128]{1,0:T(8,128)S(1)} custom-call(f32[128,128]{1,0:T(8,128)S(1)} %cholesky.267), custom_call_target="Cholesky" | custom-call | tf_op jit(solution)/shard_map/jit(cholesky)/cholesky | solution.py:83
  705.5 10.0 %custom-call.35 = f32[1,128,128]{1,2,0:T(8,128)S(1)} custom-call(f32[1,128,128]{2,1,0:T(8,128)S(1)} %get-tuple-element.83), custom_call_target="InvertDiagBlocksLowerTriangular" | custom-call | tf_op jit(solution)/shard_map/jit(cholesky)/cholesky | solution.py:83
  716.2 11.7 %cholesky.236 = f32[128,128]{1,0:T(8,128)S(1)} custom-call(f32[128,128]{1,0:T(8,128)S(1)} %cholesky.272), custom_call_target="Cholesky" | custom-call | tf_op jit(solution)/shard_map/jit(cholesky)/cholesky | solution.py:83
  727.9 9.8 %custom-call.36 = f32[1,128,128]{1,2,0:T(8,128)S(1)} custom-call(f32[1,128,128]{2,1,0:T(8,128)S(1)} %get-tuple-element.80), custom_call_target="InvertDiagBlocksLowerTriangular" | custom-call | tf_op jit(solution)/shard_map/jit(cholesky)/cholesky | solution.py:83
  738.4 11.9 %cholesky.253 = f32[128,128]{1,0:T(8,128)S(1)} custom-call(f32[128,128]{1,0:T(8,128)S(1)} %convolution_subtract_fusion.8), custom_call_target="Cholesky" | custom-call | tf_op jit(solution)/shard_map/jit(cholesky)/cholesky | solution.py:83
  754.9 7.7 while.1
  755.6 1.3 bitcast_dynamic-update-slice_fusion.3
  757.5 1.3 bitcast_dynamic-update-slice_fusion.3
  759.4 1.3 bitcast_dynamic-update-slice_fusion.3
  761.3 1.3 bitcast_dynamic-update-slice_fusion.3
  762.6 39.3 %custom-call.37 = f32[4,128,128]{1,2,0:T(8,128)S(1)} custom-call(f32[4,128,128]{2,1,0:T(8,128)S(1)} %get-tuple-element.52), custom_call_target="InvertDiagBlocksLowerTriangular" | custom-call | tf_op jit(solution)/shard_map/jit(_cho_solve)/triangular_solve | solution.py:84
  (81 shorter events, 18.1 us)
Async XLA Ops:
  7.2 82.3 %copy-start = (bf16[1,512,128]{2,1,0:T(8,128)(2,1)S(1)}, bf16[1,512,128]{2,1,0:T(8,128)(2,1)}, u32[]{:S(2)}) copy-start(bf16[1,512,128]{2,1,0:T(8,128)(2,1)} %param.7) | copy-start | bytes 393220
  7.2 506.4 %all-reduce.10.cloned.1.call-start = ((), (), s32[]{:S(2)}) async-start(), calls=%async_computation | async-start | bytes 524288
  7.2 0.7 copy-start.5
  64.4 0.7 copy-start.6
  66.3 0.7 copy-start.4
  229.9 0.9 copy-start.7
  231.9 0.7 copy-start.3
  231.9 436.7 %all-reduce.12.cloned.1.call-start = ((), (), s32[]{:S(2)}) async-start(), calls=%async_computation.1 | async-start | bytes 2621440 | tf_op jit(solution)/shard_map/psum | solution.py:119
  669.9 1.2 copy-start.1
  754.8 47.1 %copy-start.2 = (f32[512,128]{1,0:T(8,128)S(1)}, f32[512,128]{1,0:T(8,128)}, u32[]{:S(2)}) copy-start(f32[512,128]{1,0:T(8,128)} %get-tuple-element.72) | copy-start | bytes 786436
Sparse Core Ops, SparseCore 0:
  232.0 146.0 all-reduce.9
  515.5 153.0 all-reduce.11
where the time goes:
time: 814 us
  blocking collectives  496 us (61%)
  waiting for transfers between devices  152 us (19%)
  other arithmetic  123 us (15%)
  between operations  18.3 us (2%)
  local copies, waits for them, and re-layouts  14.2 us (2%)
  matrix products  10.6 us (1%)
    unnamed x2, blocking collectives  299 us
    psum x1, waiting for transfers between devices, shards(): gram_sum, cross_sum = lax.psum((gram_part, cross_part), 'pos')  152 us
    pmax x1, blocking collectives, shards(): row_top = lax.pmax(maxima, 'pos')  140 us
    another operation x14, other arithmetic, ridge_solve(): factor_low = jnp.linalg.cholesky(gram_sum + RIDGE * identity)  78.8 us
    all_gather x1, blocking collectives, shards(): lax.all_gather(ref_queries, 'pos', axis=1, tiled=True)  56.5 us
    another operation x3, other arithmetic, ridge_solve(): return jax.scipy.linalg.cho_solve((factor_low, True), cross_sum)  39.4 us
  transfers between devices with their start and end apart: 2, of which 1 were waited for; matrix products, arithmetic and copies ran while one was open for 1% of the time, Pallas kernels for 0%

commit v1 on v0

v1 whole, which is shorter than its diff:
```python
import math

import jax
import jax.numpy as jnp
from jax import lax
from jax.experimental import pallas as pl
from jax.experimental.pallas import tpu as pltpu
from jax.sharding import PartitionSpec as P

RIDGE = 1.0
NEG_FILL = -1e30
RING = 8
BLOCK = 512
DH = 128
LANES = 128
CHUNKS = BLOCK // LANES
SLAB = DH // RING
INV_ROOT = 1.0 / math.sqrt(DH)
MESH_ID = pl.DeviceIdType.MESH
F32 = jnp.float32
BF16 = jnp.bfloat16


def dot(a, b, ca, cb, precision=None):
    return lax.dot_general(a, b, (((ca,), (cb,)), ((), ())), precision=precision, preferred_element_type=F32)


def chunk(c):
    return slice(c * LANES, (c + 1) * LANES)


def exchange_kernel(
    qpos_ref, q_ref, k_ref, v_ref, slots_ref,
    q_out, qp_out, ct_out, ot_out, own_out,
    q_y, q_z, qp_y, qp_z, c_local, c_z, c_y, c_g, vt, n_send, n_z, s_z, n_y, s_y, o_g,
    send_sems, recv_sems,
):
    me = lax.axis_index("pos")
    y = lax.rem(me, RING)
    z = lax.div(me, RING)

    def y_peer(o):
        return {"pos": z * RING + lax.rem(y + o, RING)}

    def z_peer(o):
        return {"pos": lax.rem(z + o, RING) * RING + y}

    offsets = range(1, RING)
    barrier = pltpu.get_barrier_semaphore()
    for o in offsets:
        pl.semaphore_signal(barrier, inc=1, device_id=y_peer(o), device_id_type=MESH_ID)
        pl.semaphore_signal(barrier, inc=1, device_id=z_peer(o), device_id_type=MESH_ID)

    base = me * BLOCK
    position = lax.broadcasted_iota(jnp.int32, (BLOCK, BLOCK), 0) + base
    one_hot = jnp.where(position == slots_ref[...], 1.0, 0.0).astype(BF16)
    c_local[...] = dot(k_ref[...], one_hot, 0, 0).astype(BF16).reshape(RING, SLAB, BLOCK)
    q_y[y] = q_ref[...].astype(F32)
    lane_id = lax.broadcasted_iota(jnp.int32, (RING, LANES), 0) * LANES + lax.broadcasted_iota(jnp.int32, (RING, LANES), 1)
    tile = jnp.zeros((RING, LANES), jnp.int32)
    for i in range(RING):
        tile = jnp.where(lane_id == me * RING + i, qpos_ref[0, i], tile)
    qp_y[0] = tile
    vt[...] = v_ref[...].astype(F32).T.astype(BF16)

    started = []

    def send(stream, o, src, dst, peer):
        copy = pltpu.make_async_remote_copy(
            src_ref=src, dst_ref=dst, send_sem=send_sems.at[stream, o], recv_sem=recv_sems.at[stream, o],
            device_id=peer, device_id_type=MESH_ID,
        )
        copy.start()
        started.append(copy)
        return copy

    def arrive(copies):
        for copy in copies:
            copy.wait_recv()

    pl.semaphore_wait(barrier, 2 * (RING - 1))

    get_q = [send(0, o, q_y.at[y], q_y.at[y], y_peer(o)) for o in offsets]
    get_qp = [send(1, o, qp_y.at[0], qp_y.at[o], y_peer(o)) for o in offsets]
    get_c = [send(2, o, c_local.at[lax.rem(z + o, RING)], c_z.at[o], z_peer(o)) for o in offsets]

    arrive(get_q)
    q_z[z] = q_y[...].reshape(RING * RING, DH).astype(BF16)
    get_q = [send(3, o, q_z.at[z], q_z.at[z], z_peer(o)) for o in offsets]
    arrive(get_qp)
    qp_z[0] = sum((qp_y[o] for o in offsets), qp_y[0])
    get_qp = [send(4, o, qp_z.at[0], qp_z.at[o], z_peer(o)) for o in offsets]

    arrive(get_c)
    c_y[0] = sum((c_z[o].astype(F32) for o in offsets), c_local[z].astype(F32)).astype(BF16)
    get_c = [send(5, o, c_y.at[0], c_y.at[o], y_peer(o)) for o in offsets]

    arrive(get_q)
    arrive(get_qp)
    qp = sum((qp_z[o] for o in offsets), qp_z[0])
    qp_out[...] = qp
    q_out[...] = q_z[...].reshape(BLOCK, DH)

    arrive(get_c)
    c_g[z] = sum((c_y[o].astype(F32) for o in offsets), c_y[0].astype(F32)).astype(BF16)
    get_c = [send(6, o, c_g.at[z], c_g.at[z], z_peer(o)) for o in offsets]

    key_pos = lax.broadcasted_iota(jnp.int32, (BLOCK, LANES), 0) + base
    tops, totals = [], []
    for c in range(CHUNKS):
        scores = dot(k_ref[...], q_out[chunk(c), :], 1, 1) * INV_ROOT
        allowed = key_pos <= qp[c:c + 1, :]
        masked = jnp.where(allowed, scores, NEG_FILL)
        top = jnp.max(masked, axis=0, keepdims=True)
        weights = jnp.where(allowed, jnp.exp(masked - top), 0.0)
        tops.append(top)
        totals.append(jnp.sum(weights, axis=0, keepdims=True))
        n_send[:, :, chunk(c)] = dot(vt[...], weights.astype(BF16), 1, 0).reshape(RING, SLAB, LANES)
    s_z[0] = jnp.concatenate(tops + totals, axis=0)

    get_s = [send(7, o, s_z.at[0], s_z.at[o], z_peer(o)) for o in offsets]
    get_n = [send(8, o, n_send.at[lax.rem(z + o, RING)], n_z.at[o], z_peer(o)) for o in offsets]

    def merge(stats, first, others):
        top_of = stats[0][:CHUNKS]
        for tile in stats[1:]:
            top_of = jnp.maximum(top_of, tile[:CHUNKS])
        scales = [jnp.exp(tile[:CHUNKS] - top_of) for tile in stats]
        total_of = sum(s * tile[CHUNKS:] for s, tile in zip(scales, stats))
        numers = []
        for c in range(CHUNKS):
            numer = first[:, chunk(c)] * scales[0][c:c + 1]
            for o in offsets:
                numer = numer + others[o, :, chunk(c)] * scales[o][c:c + 1]
            numers.append(numer)
        return top_of, total_of, numers

    arrive(get_s)
    arrive(get_n)
    top_z, total_z, numer_z = merge([s_z[o] for o in range(RING)], n_send.at[z], n_z)
    s_y[0] = jnp.concatenate([top_z, total_z], axis=0)
    for c in range(CHUNKS):
        n_y[0, :, chunk(c)] = numer_z[c]
    get_s = [send(9, o, s_y.at[0], s_y.at[o], y_peer(o)) for o in offsets]
    get_n = [send(10, o, n_y.at[0], n_y.at[o], y_peer(o)) for o in offsets]

    arrive(get_s)
    arrive(get_n)
    _, total, numer = merge([s_y[o] for o in range(RING)], n_y.at[0], n_y)
    for c in range(CHUNKS):
        o_g[z, :, chunk(c)] = (numer[c] / total[c:c + 1]).astype(BF16)
    get_o = [send(11, o, o_g.at[z], o_g.at[z], z_peer(o)) for o in offsets]

    arrive(get_c)
    ct_out[...] = c_g[...].reshape(DH, BLOCK)
    arrive(get_o)
    attended = o_g[...].reshape(DH, BLOCK)
    ot_out[...] = attended
    own_row = lax.broadcasted_iota(jnp.int32, (RING, BLOCK), 0) + me * RING
    pick = jnp.where(lax.broadcasted_iota(jnp.int32, (RING, BLOCK), 1) == own_row, 1.0, 0.0).astype(BF16)
    own_out[...] = dot(pick, attended, 1, 1).astype(BF16)
    for copy in started:
        copy.wait_send()


STREAMS = 12


def exchange(queries, qpos, keys, values, slots):
    vmem = pl.BlockSpec(memory_space=pltpu.VMEM)
    table = pltpu.VMEM((RING, SLAB, BLOCK), BF16)
    wide = pltpu.VMEM((RING, SLAB, BLOCK), F32)
    return pl.pallas_call(
        exchange_kernel,
        out_shape=(
            jax.ShapeDtypeStruct((BLOCK, DH), BF16),
            jax.ShapeDtypeStruct((RING, LANES), jnp.int32),
            jax.ShapeDtypeStruct((DH, BLOCK), BF16),
            jax.ShapeDtypeStruct((DH, BLOCK), BF16),
            jax.ShapeDtypeStruct((RING, DH), BF16),
        ),
        in_specs=[pl.BlockSpec(memory_space=pltpu.SMEM), vmem, vmem, vmem, vmem],
        out_specs=(vmem,) * 5,
        scratch_shapes=[
            pltpu.VMEM((RING, RING, DH), F32),
            pltpu.VMEM((RING, RING * RING, DH), BF16),
            pltpu.VMEM((RING, RING, LANES), jnp.int32),
            pltpu.VMEM((RING, RING, LANES), jnp.int32),
            table, table, table, table,
            pltpu.VMEM((DH, BLOCK), BF16),
            wide, wide,
            pltpu.VMEM((RING, 2 * CHUNKS, LANES), F32),
            wide,
            pltpu.VMEM((RING, 2 * CHUNKS, LANES), F32),
            table,
            pltpu.SemaphoreType.DMA((STREAMS, RING)),
            pltpu.SemaphoreType.DMA((STREAMS, RING)),
        ],
        compiler_params=pltpu.CompilerParams(collective_id=0, has_side_effects=True),
        name="exchange",
    )(qpos, queries, keys, values, slots)


def invert_spd(a):
    n = a.shape[0]
    row_id = lax.broadcasted_iota(jnp.int32, (8, n), 0)
    lane = lax.broadcasted_iota(jnp.int32, (8, n), 1)
    rows = [a[8 * g:8 * g + 8, :] for g in range(n // 8)]
    for k in range(0, n, 4):
        g0, s0 = divmod(k, 8)
        pivot = rows[g0]
        cols = [[jnp.broadcast_to(r[:, k + b:k + b + 1], (8, n)) for b in range(4)] for r in rows]

        def entry(i, j):
            return jnp.broadcast_to(cols[g0][j][s0 + i:s0 + i + 1, :], (8, n))

        p = {(i, j): entry(i, j) for i in range(4) for j in range(i + 1)}
        d0 = 1.0 / (p[0, 0] * p[1, 1] - p[1, 0] * p[1, 0])
        i00, i11, i10 = p[1, 1] * d0, p[0, 0] * d0, -p[1, 0] * d0
        t00, t01 = p[2, 0] * i00 + p[2, 1] * i10, p[2, 0] * i10 + p[2, 1] * i11
        t10, t11 = p[3, 0] * i00 + p[3, 1] * i10, p[3, 0] * i10 + p[3, 1] * i11
        s00 = p[2, 2] - (t00 * p[2, 0] + t01 * p[2, 1])
        s10 = p[3, 2] - (t10 * p[2, 0] + t11 * p[2, 1])
        s11 = p[3, 3] - (t10 * p[3, 0] + t11 * p[3, 1])
        d1 = 1.0 / (s00 * s11 - s10 * s10)
        j00, j11, j10 = s11 * d1, s00 * d1, -s10 * d1
        w = [jnp.broadcast_to(pivot[s0 + i:s0 + i + 1, :], (8, n)) for i in range(4)]
        w = [jnp.where(lane == k + i, 1.0, jnp.where((lane >= k) & (lane < k + 4), 0.0, w[i])) for i in range(4)]
        u2 = w[2] - (t00 * w[0] + t01 * w[1])
        u3 = w[3] - (t10 * w[0] + t11 * w[1])
        x2 = j00 * u2 + j10 * u3
        x3 = j10 * u2 + j11 * u3
        v0 = w[0] - (p[2, 0] * x2 + p[3, 0] * x3)
        v1 = w[1] - (p[2, 1] * x2 + p[3, 1] * x3)
        x0 = i00 * v0 + i10 * v1
        x1 = i10 * v0 + i11 * v1
        x = [x0, x1, x2, x3]
        own_cols = (lane >= k) & (lane < k + 4)
        new_rows = []
        for g, r in enumerate(rows):
            kept = jnp.where(own_cols, 0.0, r)
            new = kept - ((cols[g][0] * x[0] + cols[g][1] * x[1]) + (cols[g][2] * x[2] + cols[g][3] * x[3]))
            if g == g0:
                for i in range(4):
                    new = jnp.where(row_id == s0 + i, x[i], new)
            new_rows.append(new)
        rows = new_rows
    return jnp.concatenate(rows, axis=0)


def fit_kernel(q_ref, qp_ref, ct_ref, ot_ref, slots_ref, fitted_ref, feats, gram):
    keys = ct_ref[...].astype(F32).T.astype(BF16)
    slot_col = jnp.concatenate(
        [jnp.broadcast_to(slots_ref[:, chunk(c)], (LANES, LANES)).T for c in range(CHUNKS)], axis=0
    )
    for c in range(CHUNKS):
        logits = dot(keys, q_ref[chunk(c), :], 1, 1) * INV_ROOT
        allowed = slot_col <= qp_ref[c:c + 1, :]
        masked = jnp.where(allowed, logits, NEG_FILL)
        top = jnp.max(masked, axis=0, keepdims=True)
        raw = jnp.where(allowed, jnp.exp(masked - top), 0.0)
        feats[:, chunk(c)] = (raw / jnp.sum(raw, axis=0, keepdims=True)).astype(BF16)
    ft = feats[...]
    gram[:, :BLOCK] = dot(ft, ft, 1, 1)
    diagonal = lax.broadcasted_iota(jnp.int32, (LANES, LANES), 0) == lax.broadcasted_iota(jnp.int32, (LANES, LANES), 1)
    for c in range(CHUNKS):
        gram[chunk(c), chunk(c)] = gram[chunk(c), chunk(c)] + jnp.where(diagonal, RIDGE, 0.0)
    gram[:, BLOCK:] = ft.astype(F32)

    def eliminate(b, carry):
        rows = pl.ds(pl.multiple_of(b * LANES, LANES), LANES)
        inverse = invert_spd(gram[rows, rows])
        panel = dot(inverse, gram[rows, :], 1, 0, lax.Precision.HIGHEST)
        for c in range(CHUNKS):
            @pl.when(b == c)
            def _():
                gram[chunk(c), :] = panel

            @pl.when(b != c)
            def _():
                gram[chunk(c), :] = gram[chunk(c), :] - dot(gram[chunk(c), rows], panel, 1, 0, lax.Precision.HIGHEST)
        return carry

    lax.fori_loop(0, CHUNKS, eliminate, 0)
    solved = gram[:, BLOCK:]
    high = solved.astype(BF16)
    low = (solved - high.astype(F32)).astype(BF16)
    attended = ot_ref[...]
    fitted_ref[...] = dot(high, attended, 1, 1) + dot(low, attended, 1, 1)


def fit(queries, qp, ct, ot, slots):
    vmem = pl.BlockSpec(memory_space=pltpu.VMEM)
    return pl.pallas_call(
        fit_kernel,
        out_shape=jax.ShapeDtypeStruct((BLOCK, DH), F32),
        in_specs=[vmem] * 5,
        out_specs=vmem,
        scratch_shapes=[pltpu.VMEM((BLOCK, BLOCK), BF16), pltpu.VMEM((BLOCK, 2 * BLOCK), F32)],
        name="fit",
    )(queries, qp, ct, ot, slots)


def shards(ref_queries, query_pos, cache_keys, cache_values, slot_index):
    queries, qp, ct, ot, own = exchange(
        ref_queries[0], query_pos, cache_keys[0], cache_values[0], slot_index
    )
    fitted = fit(queries, qp, ct, ot, slot_index)
    return (own[None], fitted[None])


def solution(mesh):
    in_specs = (
        P("head", "pos", None),
        P("head", "pos"),
        P("head", "pos", None),
        P("head", "pos", None),
        P("head", None),
    )
    out_specs = (P("head", "pos", None), P("head", None, None))
    return jax.shard_map(shards, mesh=mesh, in_specs=in_specs, out_specs=out_specs, check_vma=False)
```

time: 814 us -> 96.4 us (0.12)
  blocking collectives: 496 us -> 0 us
  waiting for transfers between devices: 152 us -> 0 us
  other arithmetic: 123 us -> 0 us
  Pallas kernels: 0 us -> 95.1 us
  between operations: 18.3 us -> 0.65 us
  local copies, waits for them, and re-layouts: 14.2 us -> 0.58 us
  matrix products: 10.6 us -> 0 us
    unnamed x2 -> x0, blocking collectives: 299 us -> none
    psum x1 -> x0, waiting for transfers between devices: 152 us -> none  [shards(): gram_sum, cross_sum = lax.psum((gram_part, cross_part), 'pos')]
    pmax x1 -> x0, blocking collectives: 140 us -> none  [shards(): row_top = lax.pmax(maxima, 'pos')]
    another operation x17 -> x0, other arithmetic: 118 us -> none  [the longest x14 78.8 us: ridge_solve(): factor_low = jnp.linalg.cholesky(gram_sum + RIDGE * identity)]
    pallas_call x0 -> x2, Pallas kernels: none -> 95.1 us  [the longest x1 52.1 us: exchange(): pl.pallas_call(exchange_kernel, out_shape=(jax.ShapeDtypeStruct((BLOCK, D...]
    all_gather x1 -> x0, blocking collectives: 56.5 us -> none  [shards(): lax.all_gather(ref_queries, 'pos', axis=1, tiled=True)]
  transfers between devices with their start and end apart: 2 -> 0, of which waited for: 1 -> 0; matrix products, arithmetic and copies ran while one was open for 1% -> 0% of each run, Pallas kernels for 0% -> 0%
where the time goes in v1:
time: 96.4 us; the launch traced here: 96.3 us
  Pallas kernels  95.1 us (99%)
    pallas_call x1, Pallas kernels, exchange(): pl.pallas_call(exchange_kernel, out_shape=(jax.ShapeDtypeStruct((BLOCK, D...  52.1 us
    pallas_call x1, Pallas kernels, fit(): pl.pallas_call(fit_kernel, out_shape=jax.ShapeDtypeStruct((BLOCK, DH), F3...  43 us

profile of v1, /device:TPU:6, one launch (start us, length us, event | category | flops | bytes accessed | tf_op | source)
XLA Modules:
  0.0 96.3 jit_solution(16162319646136960127)
XLA Ops:
  0.6 52.1 %exchange.1 = (bf16[512,128]{1,0:T(8,128)(2,1)}, s32[8,128]{1,0:T(8,128)}, bf16[128,512]{1,0:T(8,128)(2,1)}, bf16[128,512]{1,0:T(8,128)(2,1)}, bf16[8,128]{1,0:T(8,128)(2,1)}) custom-call(s32[1,8]{1,0:T(1,128)} %qpos_ref.1, bf16[8,128]{1,0:T(8,128)(2,1)} %bitcast.8, bf16[512,128]{1,0:T(8,128)(2,1)} %bitcast.6, bf16[512,128]{1,0:T(8,128)(2,1)} %bitcast.7, ...), custom_call_target="tpu_custom_call" | custom-call | tf_op jit(solution)/shard_map/exchange/pallas_call | solution.py:173
  52.7 0.0 copy-start
  52.7 43.0 %fit.1 = f32[512,128]{1,0:T(8,128)} custom-call(bf16[512,128]{1,0:T(8,128)(2,1)} %get-tuple-element.8.q_ref, s32[8,128]{1,0:T(8,128)} %get-tuple-element.9.qp_ref, bf16[128,512]{1,0:T(8,128)(2,1)} %get-tuple-element.10.ct_ref, bf16[128,512]{1,0:T(8,128)(2,1)} %get-tuple-element.11.ot_ref, s32[1,512]{1,0:T(1,128)} %slots_ref.3), custom_call_target="tpu_custom_call" | custom-call | tf_op jit(solution)/shard_map/fit/pallas_call | solution.py:294
  95.7 0.0 copy-done
  95.7 0.6 copy.8
Async XLA Ops:
  52.7 43.0 %copy-start = (bf16[8,128]{1,0:T(8,128)(2,1)S(1)}, bf16[8,128]{1,0:T(8,128)(2,1)}, u32[]{:S(2)}) copy-start(bf16[8,128]{1,0:T(8,128)(2,1)} %get-tuple-element.7) | copy-start | bytes 6148

commit v2 on v1

v2 whole, which is shorter than its diff:
```python
import math

import jax
import jax.numpy as jnp
from jax import lax
from jax.experimental import pallas as pl
from jax.experimental.pallas import tpu as pltpu
from jax.sharding import PartitionSpec as P

RIDGE = 1.0
NEG_FILL = -1e30
RING = 8
BLOCK = 512
DH = 128
LANES = 128
CHUNKS = BLOCK // LANES
SLAB = DH // RING
INV_ROOT = 1.0 / math.sqrt(DH)
MESH_ID = pl.DeviceIdType.MESH
F32 = jnp.float32
BF16 = jnp.bfloat16


def dot(a, b, ca, cb, precision=None):
    return lax.dot_general(a, b, (((ca,), (cb,)), ((), ())), precision=precision, preferred_element_type=F32)


def chunk(c):
    return slice(c * LANES, (c + 1) * LANES)


def exact(a, b, ca, cb):
    return dot(a, b, ca, cb, lax.Precision.HIGHEST)


def invert_spd(a):
    n = a.shape[0]
    sub = lax.broadcasted_iota(jnp.int32, (8, n), 0)
    lane = lax.broadcasted_iota(jnp.int32, (8, n), 1)

    def along(v, j):
        return jnp.broadcast_to(v[:, j:j + 1], (8, n))

    def down(v, i):
        return jnp.broadcast_to(v[i:i + 1, :], (8, n))

    rows = [a[8 * g:8 * g + 8, :] for g in range(n // 8)]
    for g0 in range(n // 8):
        k = 8 * g0
        m = [jnp.where(lane < n + j, along(rows[g0], k + j), 0.0) for j in range(8)]
        for t in range(0, 8, 2):
            p00, p10, p11 = down(m[t], t), down(m[t], t + 1), down(m[t + 1], t + 1)
            scale = 1.0 / (p00 * p11 - p10 * p10)
            i00, i11, i10 = p11 * scale, p00 * scale, -(p10 * scale)
            new = []
            for j in range(8):
                if j == t:
                    kept, x0, x1 = None, i00, i10
                elif j == t + 1:
                    kept, x0, x1 = None, i10, i11
                else:
                    w0, w1 = down(m[j], t), down(m[j], t + 1)
                    kept, x0, x1 = m[j], i00 * w0 + i10 * w1, i10 * w0 + i11 * w1
                taken = m[t] * x0 + m[t + 1] * x1
                rest = -taken if kept is None else kept - taken
                new.append(jnp.where(sub == t, x0, jnp.where(sub == t + 1, x1, rest)))
            m = new
        own = (lane >= k) & (lane < k + 8)
        w = jnp.where(own, jnp.where(lane - k == sub, 1.0, 0.0), rows[g0])
        terms = [m[j] * down(w, j) for j in range(8)]
        while len(terms) > 1:
            terms = [u + v for u, v in zip(terms[::2], terms[1::2])]
        x = terms[0]
        xs = [down(x, j) for j in range(8)]
        updated = []
        for g, r in enumerate(rows):
            if g == g0:
                updated.append(x)
                continue
            terms = [along(r, k + j) * xs[j] for j in range(8)]
            while len(terms) > 1:
                terms = [u + v for u, v in zip(terms[::2], terms[1::2])]
            updated.append(jnp.where(own, 0.0, r) - terms[0])
        rows = updated
    return jnp.concatenate(rows, axis=0)


def compaction_kernel(
    qpos_hbm, q_hbm, k_hbm, v_hbm, slots_hbm,
    own_out, fitted_ref,
    qpos_ref, q_ref, k_ref, v_ref, slots_ref,
    q_y, q_z, qp_y, qp_z, c_local, c_z, c_y, c_g, vt, n_send, n_z, s_z, n_y, s_y, o_g,
    feats, gram, inverse, lower, upper,
    load_sems, send_sems, recv_sems,
):
    me = lax.axis_index("pos")
    y = lax.rem(me, RING)
    z = lax.div(me, RING)

    def y_peer(o):
        return {"pos": z * RING + lax.rem(y + o, RING)}

    def z_peer(o):
        return {"pos": lax.rem(z + o, RING) * RING + y}

    offsets = range(1, RING)
    barrier = pltpu.get_barrier_semaphore()
    for o in offsets:
        pl.semaphore_signal(barrier, inc=1, device_id=y_peer(o), device_id_type=MESH_ID)
        pl.semaphore_signal(barrier, inc=1, device_id=z_peer(o), device_id_type=MESH_ID)

    loads = [
        pltpu.make_async_copy(src, dst, load_sems.at[i])
        for i, (src, dst) in enumerate([
            (slots_hbm, slots_ref), (k_hbm, k_ref), (qpos_hbm, qpos_ref), (q_hbm, q_ref), (v_hbm, v_ref),
        ])
    ]
    for load in loads:
        load.start()
    for load in loads[:4]:
        load.wait()

    base = me * BLOCK
    position = lax.broadcasted_iota(jnp.int32, (BLOCK, BLOCK), 0) + base
    one_hot = jnp.where(position == slots_ref[...], 1.0, 0.0).astype(BF16)
    c_local[...] = dot(k_ref[...], one_hot, 0, 0).astype(BF16).reshape(RING, SLAB, BLOCK)
    q_y[y] = q_ref[...].astype(F32)
    lane_id = lax.broadcasted_iota(jnp.int32, (RING, LANES), 0) * LANES + lax.broadcasted_iota(jnp.int32, (RING, LANES), 1)
    tile = jnp.zeros((RING, LANES), jnp.int32)
    for i in range(RING):
        tile = jnp.where(lane_id == me * RING + i, qpos_ref[0, i], tile)
    qp_y[0] = tile
    loads[4].wait()
    vt[...] = v_ref[...].astype(F32).T.astype(BF16)

    started = []

    def copy_of(stream, o, src, dst, peer):
        return pltpu.make_async_remote_copy(
            src_ref=src, dst_ref=dst, send_sem=send_sems.at[stream, o], recv_sem=recv_sems.at[stream, o],
            device_id=peer, device_id_type=MESH_ID,
        )

    def send(stream, o, src, dst, peer):
        copy = copy_of(stream, o, src, dst, peer)
        copy.start()
        started.append(copy)
        return copy

    def arrive(copies):
        for copy in copies:
            copy.wait_recv()

    pl.semaphore_wait(barrier, 2 * (RING - 1))

    get_q = [send(0, o, q_y.at[y], q_y.at[y], y_peer(o)) for o in offsets]
    get_qp = [send(1, o, qp_y.at[0], qp_y.at[o], y_peer(o)) for o in offsets]
    get_c = [send(2, o, c_local.at[lax.rem(z + o, RING)], c_z.at[o], z_peer(o)) for o in offsets]

    arrive(get_q)
    q_z[z] = q_y[...].reshape(RING * RING, DH).astype(BF16)
    get_q = [send(3, o, q_z.at[z], q_z.at[z], z_peer(o)) for o in offsets]
    arrive(get_qp)
    qp_z[0] = sum((qp_y[o] for o in offsets), qp_y[0])
    get_qp = [send(4, o, qp_z.at[0], qp_z.at[o], z_peer(o)) for o in offsets]

    arrive(get_c)
    c_y[0] = sum((c_z[o].astype(F32) for o in offsets), c_local[z].astype(F32)).astype(BF16)
    get_c = [send(5, o, c_y.at[0], c_y.at[o], y_peer(o)) for o in offsets]

    arrive(get_q)
    arrive(get_qp)
    qp = sum((qp_z[o] for o in offsets), qp_z[0])
    queries = q_z[...].reshape(BLOCK, DH)

    arrive(get_c)
    c_g[z] = sum((c_y[o].astype(F32) for o in offsets), c_y[0].astype(F32)).astype(BF16)
    get_c = [send(6, o, c_g.at[z], c_g.at[z], z_peer(o)) for o in offsets]

    key_pos = lax.broadcasted_iota(jnp.int32, (BLOCK, LANES), 0) + base
    tops, totals = [], []
    for c in range(CHUNKS):
        scores = dot(k_ref[...], queries[chunk(c), :], 1, 1) * INV_ROOT
        allowed = key_pos <= qp[c:c + 1, :]
        masked = jnp.where(allowed, scores, NEG_FILL)
        top = jnp.max(masked, axis=0, keepdims=True)
        weights = jnp.where(allowed, jnp.exp(masked - top), 0.0)
        tops.append(top)
        totals.append(jnp.sum(weights, axis=0, keepdims=True))
        n_send[:, :, chunk(c)] = dot(vt[...], weights.astype(BF16), 1, 0).reshape(RING, SLAB, LANES)
    s_z[0] = jnp.concatenate(tops + totals, axis=0)

    get_s = [send(7, o, s_z.at[0], s_z.at[o], z_peer(o)) for o in offsets]
    get_n = [send(8, o, n_send.at[lax.rem(z + o, RING)], n_z.at[o], z_peer(o)) for o in offsets]

    def merge(stats, first, others):
        top_of = stats[0][:CHUNKS]
        for tile in stats[1:]:
            top_of = jnp.maximum(top_of, tile[:CHUNKS])
        scales = [jnp.exp(tile[:CHUNKS] - top_of) for tile in stats]
        total_of = sum(s * tile[CHUNKS:] for s, tile in zip(scales, stats))
        numers = []
        for c in range(CHUNKS):
            numer = first[:, chunk(c)] * scales[0][c:c + 1]
            for o in offsets:
                numer = numer + others[o, :, chunk(c)] * scales[o][c:c + 1]
            numers.append(numer)
        return top_of, total_of, numers

    arrive(get_c)
    compact = c_g[...].reshape(DH, BLOCK).astype(F32).T.astype(BF16)
    slot_col = jnp.concatenate(
        [jnp.broadcast_to(slots_ref[:, chunk(c)], (LANES, LANES)).T for c in range(CHUNKS)], axis=0
    )
    for c in range(CHUNKS):
        logits = dot(compact, queries[chunk(c), :], 1, 1) * INV_ROOT
        allowed = slot_col <= qp[c:c + 1, :]
        masked = jnp.where(allowed, logits, NEG_FILL)
        top = jnp.max(masked, axis=0, keepdims=True)
        raw = jnp.where(allowed, jnp.exp(masked - top), 0.0)
        feats[:, chunk(c)] = (raw * (1.0 / jnp.sum(raw, axis=0, keepdims=True))).astype(BF16)
    diagonal = lax.broadcasted_iota(jnp.int32, (LANES, LANES), 0) == lax.broadcasted_iota(jnp.int32, (LANES, LANES), 1)
    for i in range(CHUNKS):
        for j in range(i + 1):
            block = dot(feats[chunk(i), :], feats[chunk(j), :], 1, 1)
            gram[i, j] = block + jnp.where(diagonal, RIDGE, 0.0) if i == j else block

    def merge_z():
        arrive(get_s)
        arrive(get_n)
        top_z, total_z, numer_z = merge([s_z[o] for o in range(RING)], n_send.at[z], n_z)
        s_y[0] = jnp.concatenate([top_z, total_z], axis=0)
        for c in range(CHUNKS):
            n_y[0, :, chunk(c)] = numer_z[c]
        for o in offsets:
            copy_of(9, o, s_y.at[0], s_y.at[o], y_peer(o)).start()
            copy_of(10, o, n_y.at[0], n_y.at[o], y_peer(o)).start()

    def merge_y():
        for o in offsets:
            copy_of(9, o, s_y.at[0], s_y.at[o], y_peer(o)).wait()
            copy_of(10, o, n_y.at[0], n_y.at[o], y_peer(o)).wait()
        _, total, numer = merge([s_y[o] for o in range(RING)], n_y.at[0], n_y)
        for c in range(CHUNKS):
            o_g[z, :, chunk(c)] = (numer[c] / total[c:c + 1]).astype(BF16)
        for o in offsets:
            copy_of(11, o, o_g.at[z], o_g.at[z], z_peer(o)).start()

    def eliminate(b, carry):
        inverse[b] = invert_spd(gram[b, b])
        for c in range(CHUNKS - 1):
            @pl.when(b == c)
            def _():
                for i in range(c + 1, CHUNKS):
                    lower[i, c] = exact(gram[i, c], inverse[c], 1, 0)
                    upper[c, i] = exact(inverse[c], gram[i, c], 1, 1)
                for i in range(c + 1, CHUNKS):
                    for j in range(c + 1, i + 1):
                        gram[i, j] = gram[i, j] - exact(lower[i, c], gram[j, c], 1, 1)

        pl.when(b == MERGE_Z_AFTER)(merge_z)
        pl.when(b == MERGE_Y_AFTER)(merge_y)
        return carry

    lax.fori_loop(0, CHUNKS, eliminate, 0)

    for o in offsets:
        copy_of(11, o, o_g.at[z], o_g.at[z], z_peer(o)).wait()
    attended = o_g[...].reshape(DH, BLOCK)
    own_row = lax.broadcasted_iota(jnp.int32, (RING, BLOCK), 0) + me * RING
    pick = jnp.where(lax.broadcasted_iota(jnp.int32, (RING, BLOCK), 1) == own_row, 1.0, 0.0).astype(BF16)
    own_out[...] = dot(pick, attended, 1, 1).astype(BF16)
    cross = dot(feats[...], attended, 1, 1)
    part = []
    for i in range(CHUNKS):
        rhs = cross[chunk(i), :]
        for c in range(i):
            rhs = rhs - exact(lower[i, c], part[c], 1, 0)
        part.append(rhs)
    part = [exact(inverse[i], part[i], 1, 0) for i in range(CHUNKS)]
    for c in reversed(range(CHUNKS)):
        for i in range(c + 1, CHUNKS):
            part[c] = part[c] - exact(upper[c, i], part[i], 1, 0)
        fitted_ref[chunk(c), :] = part[c]
    for copy in started:
        copy.wait_send()


STREAMS = 12
MERGE_Z_AFTER = 0
MERGE_Y_AFTER = 2


def compaction(queries, qpos, keys, values, slots):
    vmem = pl.BlockSpec(memory_space=pltpu.VMEM)
    table = pltpu.VMEM((RING, SLAB, BLOCK), BF16)
    wide = pltpu.VMEM((RING, SLAB, BLOCK), F32)
    tile = pltpu.VMEM((RING, RING, LANES), F32)
    blocks = pltpu.VMEM((CHUNKS, CHUNKS, LANES, LANES), F32)
    return pl.pallas_call(
        compaction_kernel,
        out_shape=(
            jax.ShapeDtypeStruct((RING, DH), BF16),
            jax.ShapeDtypeStruct((BLOCK, DH), F32),
        ),
        in_specs=[pl.BlockSpec(memory_space=pl.ANY)] * 5,
        out_specs=(vmem,) * 2,
        scratch_shapes=[
            pltpu.SMEM((1, RING), jnp.int32),
            pltpu.VMEM((RING, DH), BF16),
            pltpu.VMEM((BLOCK, DH), BF16),
            pltpu.VMEM((BLOCK, DH), BF16),
            pltpu.VMEM((1, BLOCK), jnp.int32),
            pltpu.VMEM((RING, RING, DH), F32),
            pltpu.VMEM((RING, RING * RING, DH), BF16),
            pltpu.VMEM((RING, RING, LANES), jnp.int32),
            pltpu.VMEM((RING, RING, LANES), jnp.int32),
            table, table, table, table,
            pltpu.VMEM((DH, BLOCK), BF16),
            wide, wide, tile, wide, tile, table,
            pltpu.VMEM((BLOCK, BLOCK), BF16),
            blocks,
            pltpu.VMEM((CHUNKS, LANES, LANES), F32),
            blocks, blocks,
            pltpu.SemaphoreType.DMA((5,)),
            pltpu.SemaphoreType.DMA((STREAMS, RING)),
            pltpu.SemaphoreType.DMA((STREAMS, RING)),
        ],
        compiler_params=pltpu.CompilerParams(collective_id=0, has_side_effects=True),
        name="compaction",
    )(qpos, queries, keys, values, slots)


def shards(ref_queries, query_pos, cache_keys, cache_values, slot_index):
    own, fitted = compaction(ref_queries[0], query_pos, cache_keys[0], cache_values[0], slot_index)
    return (own[None], fitted[None])


def solution(mesh):
    in_specs = (
        P("head", "pos", None),
        P("head", "pos"),
        P("head", "pos", None),
        P("head", "pos", None),
        P("head", None),
    )
    out_specs = (P("head", "pos", None), P("head", None, None))
    return jax.shard_map(shards, mesh=mesh, in_specs=in_specs, out_specs=out_specs, check_vma=False)
```

time: 96.4 us -> 61.4 us (0.64)
  Pallas kernels: 95.1 us -> 57.6 us
  local copies, waits for them, and re-layouts: 0.58 us -> 2.92 us
    pallas_call x2 -> x1, Pallas kernels: 95.1 us -> 57.6 us  [compaction(): pl.pallas_call(compaction_kernel, out_shape=(jax.ShapeDtypeStruct((RING,...]
    unnamed x3 -> x4, local copies, waits for them, and re-layouts: 0.58 us -> 2.92 us
where the time goes in v2:
time: 61.4 us; the launch traced here: 61.2 us
  Pallas kernels  57.6 us (94%)
  local copies, waits for them, and re-layouts  2.92 us (5%)
  between operations  0.65 us (1%)
    pallas_call x1, Pallas kernels, compaction(): pl.pallas_call(compaction_kernel, out_shape=(jax.ShapeDtypeStruct((RING,...  57.6 us
    unnamed x4, local copies, waits for them, and re-layouts  2.92 us

profile of v2, /device:TPU:6, one launch (start us, length us, event | category | flops | bytes accessed | tf_op | source)
XLA Modules:
  0.0 61.2 jit_solution(7447542459032749711)
XLA Ops:
  0.6 57.6 %compaction.1 = (bf16[8,128]{1,0:T(8,128)(2,1)}, f32[512,128]{1,0:T(8,128)}) custom-call(s32[1,8]{1,0:T(1,128)} %qpos_hbm.1, bf16[8,128]{1,0:T(8,128)(2,1)} %bitcast.8, bf16[512,128]{1,0:T(8,128)(2,1)} %bitcast.6, bf16[512,128]{1,0:T(8,128)(2,1)} %bitcast.7, s32[1,512]{1,0:T(1,128)} %slots_hbm.1), custom_call_target="tpu_custom_call" | custom-call | tf_op jit(solution)/shard_map/compaction/pallas_call | solution.py:300
  58.3 0.0 copy-start
  58.3 0.7 %copy-done = bf16[8,128]{1,0:T(8,128)(2,1)S(1)} copy-done((bf16[8,128]{1,0:T(8,128)(2,1)S(1)}, bf16[8,128]{1,0:T(8,128)(2,1)}, u32[]{:S(2)}) %copy-start) | copy-done | bytes 2072
  59.0 0.6 copy.9
  59.5 1.7 %copy.10 = f32[1,512,128]{2,1,0:T(8,128)} copy(f32[1,512,128]{2,1,0:T(8,128)} %bitcast.5) | data formatting | bytes 524288
Async XLA Ops:
  58.3 0.7 %copy-start = (bf16[8,128]{1,0:T(8,128)(2,1)S(1)}, bf16[8,128]{1,0:T(8,128)(2,1)}, u32[]{:S(2)}) copy-start(bf16[8,128]{1,0:T(8,128)(2,1)} %get-tuple-element.4) | copy-start | bytes 6148

commit v3 on v2

v3 whole, which is shorter than its diff:
```python
import math

import jax
import jax.numpy as jnp
from jax import lax
from jax.experimental import pallas as pl
from jax.experimental.pallas import tpu as pltpu
from jax.sharding import PartitionSpec as P

RIDGE = 1.0
NEG_FILL = -1e30
RING = 8
BLOCK = 512
DH = 128
LANES = 128
CHUNKS = BLOCK // LANES
SLAB = DH // RING
HALF = BLOCK // 2
QROWS = 4
INV_ROOT = 1.0 / math.sqrt(DH)
MESH_ID = pl.DeviceIdType.MESH
F32 = jnp.float32
BF16 = jnp.bfloat16


def dot(a, b, ca, cb, precision=None):
    return lax.dot_general(a, b, (((ca,), (cb,)), ((), ())), precision=precision, preferred_element_type=F32)


def chunk(c):
    return slice(c * LANES, (c + 1) * LANES)


def exact(a, b, ca, cb):
    return dot(a, b, ca, cb, lax.Precision.HIGHEST)


def tree_sum(terms):
    while len(terms) > 1:
        terms = [u + v for u, v in zip(terms[::2], terms[1::2])] + ([terms[-1]] if len(terms) % 2 else [])
    return terms[0]


def invert_spd(a):
    n = a.shape[0]
    sub = lax.broadcasted_iota(jnp.int32, (8, n), 0)
    lane = lax.broadcasted_iota(jnp.int32, (8, n), 1)

    def along(v, j):
        return jnp.broadcast_to(v[:, j:j + 1], (8, n))

    def down(v, i):
        return jnp.broadcast_to(v[i:i + 1, :], (8, n))

    rows = [a[8 * g:8 * g + 8, :] for g in range(n // 8)]
    unit, scaled = [], []
    for g0 in range(n // 8):
        k = 8 * g0
        m = [jnp.where(lane < n + j, along(rows[g0], k + j), 0.0) for j in range(8)]
        for t in range(0, 8, 2):
            p00, p10, p11 = down(m[t], t), down(m[t], t + 1), down(m[t + 1], t + 1)
            scale = 1.0 / (p00 * p11 - p10 * p10)
            i00, i11, i10 = p11 * scale, p00 * scale, -(p10 * scale)
            f0 = jnp.where(sub == t, -1.0, jnp.where(sub == t + 1, 0.0, m[t]))
            f1 = jnp.where(sub == t + 1, -1.0, jnp.where(sub == t, 0.0, m[t + 1]))
            pivots = (sub == t) | (sub == t + 1)
            new = []
            for j in range(8):
                if j == t:
                    new.append(-(f0 * i00 + f1 * i10))
                elif j == t + 1:
                    new.append(-(f0 * i10 + f1 * i11))
                else:
                    w0, w1 = down(m[j], t), down(m[j], t + 1)
                    x0, x1 = i00 * w0 + i10 * w1, i10 * w0 + i11 * w1
                    new.append(jnp.where(pivots, 0.0, m[j]) - (f0 * x0 + f1 * x1))
            m = new
        own = (lane >= k) & (lane < k + 8)
        w = jnp.where(own, jnp.where(lane - k == sub, 1.0, 0.0), rows[g0])
        x = tree_sum([m[j] * down(w, j) for j in range(8)])
        unit.append(jnp.where(lane < k + 8, w, 0.0))
        scaled.append(jnp.where(lane < k + 8, x, 0.0))
        if k + 8 < n:
            xs = [down(x, j) for j in range(8)]
        for g in range(g0 + 1, n // 8):
            rows[g] = jnp.where(own, 0.0, rows[g]) - tree_sum([along(rows[g], k + j) * xs[j] for j in range(8)])
    return exact(jnp.concatenate(unit, axis=0), jnp.concatenate(scaled, axis=0), 0, 0)


def compaction_kernel(
    qpos_hbm, q_hbm, k_hbm, v_hbm, slots_hbm,
    own_out, fitted_ref,
    qpos_ref, q_ref, k_ref, v_ref, slots_ref,
    q_1, q_2, qp_1, qp_2, c_0, c_1, c_2, c_3, vt, n_0, n_1, s_1, n_2, s_2, o_3, feats,
    load_sems, send_sems, recv_sems,
):
    me = lax.axis_index("pos")
    place = (lax.div(me, RING), lax.rem(me, RING))

    def peer(axis, o):
        if axis == 0:
            return {"pos": lax.rem(place[0] + o, RING) * RING + place[1]}
        return {"pos": place[0] * RING + lax.rem(place[1] + o, RING)}

    offsets = (4, 3, 5, 2, 6, 1, 7)
    barrier = pltpu.get_barrier_semaphore()
    for axis in (0, 1):
        for o in offsets:
            pl.semaphore_signal(barrier, inc=1, device_id=peer(axis, o), device_id_type=MESH_ID)

    loads = [
        pltpu.make_async_copy(src, dst, load_sems.at[i])
        for i, (src, dst) in enumerate([
            (slots_hbm, slots_ref), (k_hbm, k_ref), (qpos_hbm, qpos_ref), (q_hbm, q_ref), (v_hbm, v_ref),
        ])
    ]
    for load in loads:
        load.start()
    for load in loads[:4]:
        load.wait()

    started = []

    def send(stream, axis, o, src, dst):
        copy = pltpu.make_async_remote_copy(
            src_ref=src, dst_ref=dst, send_sem=send_sems.at[stream, o], recv_sem=recv_sems.at[stream, o],
            device_id=peer(axis, o), device_id_type=MESH_ID,
        )
        copy.start()
        started.append(copy)
        return copy

    def arrive(copies):
        for copy in copies:
            copy.wait_recv()

    halves = (0, 1)

    base = me * BLOCK
    lane_id = (
        lax.broadcasted_iota(jnp.int32, (CHUNKS, LANES), 0) * LANES
        + lax.broadcasted_iota(jnp.int32, (CHUNKS, LANES), 1)
    )
    own_id = [
        HALF * h + place[h] * (RING * QROWS) + place[1 - h] * QROWS + i for h in halves for i in range(QROWS)
    ]
    tile = jnp.zeros((CHUNKS, LANES), jnp.int32)
    for i in range(RING):
        tile = jnp.where(lane_id == own_id[i], qpos_ref[0, i], tile)
    qp_1[0] = tile
    own_q = q_ref[...].astype(F32)
    for h in halves:
        q_1[h, place[1 - h]] = own_q[QROWS * h:QROWS * h + QROWS, :]
    position = lax.broadcasted_iota(jnp.int32, (BLOCK, BLOCK), 0) + base
    one_hot = jnp.where(position == slots_ref[...], 1.0, 0.0).astype(BF16)
    picked = dot(k_ref[...], one_hot, 0, 0).astype(BF16)
    for h in halves:
        c_0[h] = picked[:, h * HALF:(h + 1) * HALF].reshape(RING, SLAB, HALF)

    pl.semaphore_wait(barrier, 2 * (RING - 1))

    get_q = [send(h, 1 - h, o, q_1.at[h, place[1 - h]], q_1.at[h, place[1 - h]]) for h in halves for o in offsets]
    get_qp = [send(2, 1, o, qp_1.at[0], qp_1.at[o]) for o in offsets]
    get_c = [send(3 + h, h, o, c_0.at[h, lax.rem(place[h] + o, RING)], c_1.at[h, o]) for o in offsets for h in halves]
    loads[4].wait()
    vt[...] = v_ref[...].astype(F32).T.astype(BF16)

    arrive(get_q)
    for h in halves:
        q_2[h, place[h]] = q_1[h].reshape(RING * QROWS, DH).astype(BF16)
    get_q = [send(5 + h, h, o, q_2.at[h, place[h]], q_2.at[h, place[h]]) for o in offsets for h in halves]
    arrive(get_qp)
    qp_2[0] = tree_sum([qp_1[o] for o in range(RING)])
    get_qp = [send(7, 0, o, qp_2.at[0], qp_2.at[o]) for o in offsets]

    arrive(get_c)
    for h in halves:
        c_2[h, 0] = tree_sum([c_0[h, place[h]].astype(F32)] + [c_1[h, o].astype(F32) for o in offsets]).astype(BF16)
    get_c = [send(8 + h, 1 - h, o, c_2.at[h, 0], c_2.at[h, o]) for o in offsets for h in halves]

    arrive(get_q)
    arrive(get_qp)
    qp = tree_sum([qp_2[o] for o in range(RING)])
    queries = q_2[...].reshape(BLOCK, DH)

    arrive(get_c)
    for h in halves:
        c_3[h, place[h]] = tree_sum([c_2[h, o].astype(F32) for o in range(RING)]).astype(BF16)
    get_c = [send(10 + h, h, o, c_3.at[h, place[h]], c_3.at[h, place[h]]) for o in offsets for h in halves]

    key_pos = lax.broadcasted_iota(jnp.int32, (BLOCK, LANES), 0) + base
    get_s, get_n = [], []
    for h in halves:
        tops, totals = [], []
        for c in (0, 1):
            scores = dot(k_ref[...], queries[chunk(2 * h + c), :], 1, 1) * INV_ROOT
            allowed = key_pos <= qp[2 * h + c:2 * h + c + 1, :]
            masked = jnp.where(allowed, scores, NEG_FILL)
            top = jnp.max(masked, axis=0, keepdims=True)
            weights = jnp.where(allowed, jnp.exp(masked - top), 0.0)
            tops.append(top)
            totals.append(jnp.sum(weights, axis=0, keepdims=True))
            n_0[h, :, :, chunk(c)] = dot(vt[...], weights.astype(BF16), 1, 0).reshape(RING, SLAB, LANES)
        s_1[h, 0] = jnp.concatenate(tops + totals, axis=0)
    for o in offsets:
        for h in halves:
            get_s.append(send(12 + h, h, o, s_1.at[h, 0], s_1.at[h, o]))
            get_n.append(send(14 + h, h, o, n_0.at[h, lax.rem(place[h] + o, RING)], n_1.at[h, o]))

    def merge(stats, first, others, c):
        top = stats[0][c:c + 1]
        for tile in stats[1:]:
            top = jnp.maximum(top, tile[c:c + 1])
        scales = [jnp.exp(tile[c:c + 1] - top) for tile in stats]
        total = tree_sum([scale * tile[2 + c:3 + c] for scale, tile in zip(scales, stats)])
        numer = tree_sum(
            [first[:, chunk(c)] * scales[0]] + [others[o, :, chunk(c)] * scales[o] for o in range(1, RING)]
        )
        return top, total, numer

    arrive(get_c)
    compact = jnp.concatenate([c_3[h].reshape(DH, HALF).astype(F32).T for h in halves], axis=0).astype(BF16)
    slot_col = jnp.concatenate(
        [jnp.broadcast_to(slots_ref[:, chunk(c)], (LANES, LANES)).T for c in range(CHUNKS)], axis=0
    )
    for c in range(CHUNKS):
        logits = dot(compact, queries[chunk(c), :], 1, 1) * INV_ROOT
        allowed = slot_col <= qp[c:c + 1, :]
        masked = jnp.where(allowed, logits, NEG_FILL)
        top = jnp.max(masked, axis=0, keepdims=True)
        raw = jnp.where(allowed, jnp.exp(masked - top), 0.0)
        feats[:, chunk(c)] = (raw * (1.0 / jnp.sum(raw, axis=0, keepdims=True))).astype(BF16)
    diagonal = lax.broadcasted_iota(jnp.int32, (LANES, LANES), 0) == lax.broadcasted_iota(jnp.int32, (LANES, LANES), 1)
    gram = {}
    for i in range(CHUNKS):
        for j in range(i + 1):
            block = dot(feats[chunk(i), :], feats[chunk(j), :], 1, 1)
            gram[i, j] = block + jnp.where(diagonal, RIDGE, 0.0) if i == j else block

    def merge_first():
        for h in halves:
            merged = [merge([s_1[h, o] for o in range(RING)], n_0[h, place[h]], n_1[h], c) for c in (0, 1)]
            s_2[h, 0] = jnp.concatenate([m[0] for m in merged] + [m[1] for m in merged], axis=0)
            for c in (0, 1):
                n_2[h, 0, :, chunk(c)] = merged[c][2]
        return (
            [send(16 + h, 1 - h, o, s_2.at[h, 0], s_2.at[h, o]) for o in offsets for h in halves]
            + [send(18 + h, 1 - h, o, n_2.at[h, 0], n_2.at[h, o]) for o in offsets for h in halves]
        )

    def merge_second():
        for h in halves:
            for c in (0, 1):
                _, total, numer = merge([s_2[h, o] for o in range(RING)], n_2[h, 0], n_2[h], c)
                o_3[h, place[h], :, chunk(c)] = (numer / total).astype(BF16)
        return [send(20 + h, h, o, o_3.at[h, place[h]], o_3.at[h, place[h]]) for o in offsets for h in halves]

    inverse, lower, upper = {}, {}, {}

    def update(i, j, c):
        gram[i, j] = gram[i, j] - exact(lower[i, c], gram[j, c], 1, 1)

    def step(c):
        inverse[c] = invert_spd(gram[c, c])
        if c + 1 < CHUNKS:
            lower[c + 1, c] = exact(gram[c + 1, c], inverse[c], 1, 0)
            update(c + 1, c + 1, c)

    def rest(c):
        for i in range(c + 2, CHUNKS):
            lower[i, c] = exact(gram[i, c], inverse[c], 1, 0)
            for j in range(c + 1, i + 1):
                update(i, j, c)
        for i in range(c + 1, CHUNKS):
            upper[c, i] = exact(inverse[c], gram[i, c], 1, 1)

    arrive(get_s)
    arrive(get_n)
    get_n = merge_first()
    step(0)
    arrive(get_n)
    get_o = merge_second()
    rest(0)
    step(1)
    rest(1)
    step(2)
    arrive(get_o)
    attended = jnp.concatenate([o_3[h].reshape(DH, HALF) for h in halves], axis=1)
    row = lax.broadcasted_iota(jnp.int32, (RING, BLOCK), 0)
    column = lax.broadcasted_iota(jnp.int32, (RING, BLOCK), 1)
    pick = jnp.zeros((RING, BLOCK), F32)
    for i in range(RING):
        pick = jnp.where((row == i) & (column == own_id[i]), 1.0, pick)
    own_out[...] = dot(pick.astype(BF16), attended, 1, 1).astype(BF16)
    rest(2)
    part = [dot(feats[chunk(i), :], attended, 1, 1) for i in range(CHUNKS)]
    for c in range(CHUNKS - 1):
        for i in range(c + 1, CHUNKS):
            part[i] = part[i] - exact(lower[i, c], part[c], 1, 0)
    last = CHUNKS - 1
    share = {}
    for c in reversed(range(last)):
        part[c] = exact(inverse[c], part[c], 1, 0)
        share[c] = -upper[c, last]
        for i in range(c + 1, last):
            part[c] = part[c] - exact(upper[c, i], part[i], 1, 0)
            share[c] = share[c] - exact(upper[c, i], share[i], 1, 0)
    step(last)
    part[last] = exact(inverse[last], part[last], 1, 0)
    fitted_ref[chunk(last), :] = part[last]
    for c in range(last):
        fitted_ref[chunk(c), :] = part[c] + exact(share[c], part[last], 1, 0)
    for copy in started:
        copy.wait_send()


STREAMS = 22


def compaction(queries, qpos, keys, values, slots):
    vmem = pl.BlockSpec(memory_space=pltpu.VMEM)
    table = pltpu.VMEM((2, RING, SLAB, HALF), BF16)
    wide = pltpu.VMEM((2, RING, SLAB, HALF), F32)
    stats = pltpu.VMEM((2, RING, CHUNKS, LANES), F32)
    return pl.pallas_call(
        compaction_kernel,
        out_shape=(
            jax.ShapeDtypeStruct((RING, DH), BF16),
            jax.ShapeDtypeStruct((BLOCK, DH), F32),
        ),
        in_specs=[pl.BlockSpec(memory_space=pltpu.HBM)] * 5,
        out_specs=(vmem,) * 2,
        scratch_shapes=[
            pltpu.SMEM((1, RING), jnp.int32),
            pltpu.VMEM((RING, DH), BF16),
            pltpu.VMEM((BLOCK, DH), BF16),
            pltpu.VMEM((BLOCK, DH), BF16),
            pltpu.VMEM((1, BLOCK), jnp.int32),
            pltpu.VMEM((2, RING, QROWS, DH), F32),
            pltpu.VMEM((2, RING, RING * QROWS, DH), BF16),
            pltpu.VMEM((RING, CHUNKS, LANES), jnp.int32),
            pltpu.VMEM((RING, CHUNKS, LANES), jnp.int32),
            table, table, table, table,
            pltpu.VMEM((DH, BLOCK), BF16),
            wide, wide, stats, wide, stats, table,
            pltpu.VMEM((BLOCK, BLOCK), BF16),
            pltpu.SemaphoreType.DMA((5,)),
            pltpu.SemaphoreType.DMA((STREAMS, RING)),
            pltpu.SemaphoreType.DMA((STREAMS, RING)),
        ],
        compiler_params=pltpu.CompilerParams(collective_id=0, has_side_effects=True, vmem_limit_bytes=VMEM_LIMIT),
        name="compaction",
    )(qpos, queries, keys, values, slots)


VMEM_LIMIT = 32 * 1024 * 1024


def shards(ref_queries, query_pos, cache_keys, cache_values, slot_index):
    own, fitted = compaction(*(
        pltpu.with_memory_space_constraint(x, pltpu.HBM)
        for x in (ref_queries[0], query_pos, cache_keys[0], cache_values[0], slot_index)
    ))
    return (own[None], fitted[None])


def solution(mesh):
    in_specs = (
        P("head", "pos", None),
        P("head", "pos"),
        P("head", "pos", None),
        P("head", "pos", None),
        P("head", None),
    )
    out_specs = (P("head", "pos", None), P("head", None, None))
    return jax.shard_map(shards, mesh=mesh, in_specs=in_specs, out_specs=out_specs, check_vma=False)
```

time: 61.4 us -> 61.9 us (level)
  Pallas kernels: 57.6 us -> 59.9 us
  local copies, waits for them, and re-layouts: 2.92 us -> 1.28 us
    pallas_call x1, Pallas kernels: 57.6 us -> 59.9 us  [compaction(): pl.pallas_call(compaction_kernel, out_shape=(jax.ShapeDtypeStruct((RING,...]
    unnamed x4 -> x2, local copies, waits for them, and re-layouts: 2.92 us -> 1.28 us
where the time goes in v3:
time: 61.9 us; the launch traced here: 61.8 us
  Pallas kernels  59.9 us (97%)
  local copies, waits for them, and re-layouts  1.28 us (2%)
  between operations  0.64 us (1%)
    pallas_call x1, Pallas kernels, compaction(): pl.pallas_call(compaction_kernel, out_shape=(jax.ShapeDtypeStruct((RING,...  59.9 us
    unnamed x2, local copies, waits for them, and re-layouts  1.28 us

profile of v3, /device:TPU:6, one launch (start us, length us, event | category | flops | bytes accessed | tf_op | source)
XLA Modules:
  0.0 61.8 jit_solution(5751982423020735096)
XLA Ops:
  0.6 59.9 %compaction.1 = (bf16[8,128]{1,0:T(8,128)(2,1)S(1)}, f32[512,128]{1,0:T(8,128)S(1)}) custom-call(s32[1,8]{1,0:T(1,128)} %qpos_hbm.1, bf16[8,128]{1,0:T(8,128)(2,1)} %bitcast.9, bf16[512,128]{1,0:T(8,128)(2,1)} %bitcast.7, bf16[512,128]{1,0:T(8,128)(2,1)} %bitcast.8, s32[1,512]{1,0:T(1,128)} %slots_hbm.1), custom_call_target="tpu_custom_call" | custom-call | tf_op jit(solution)/shard_map/compaction/pallas_call | solution.py:325
  60.5 0.6 copy.9
  61.1 0.7 %copy.10 = f32[1,512,128]{2,1,0:T(8,128)} copy(f32[1,512,128]{2,1,0:T(8,128)S(1)} %bitcast.5) | data formatting | bytes 524288

commit v4 on v3

--- a/solution.py
+++ b/solution.py
@@ -1,3 +1,4 @@
+import functools
 import math
 
 import jax
@@ -31,8 +32,21 @@
     return slice(c * LANES, (c + 1) * LANES)
 
 
+def pieces(x):
+    high = x.astype(BF16)
+    rest = x - high.astype(F32)
+    middle = rest.astype(BF16)
+    return high, middle, (rest - middle.astype(F32)).astype(BF16)
+
+
 def exact(a, b, ca, cb):
-    return dot(a, b, ca, cb, lax.Precision.HIGHEST)
+    ah, am, al = pieces(a)
+    bh, bm, bl = pieces(b)
+
+    def stacked(a0, b0, a1, b1):
+        return dot(jnp.concatenate([a0, a1], axis=ca), jnp.concatenate([b0, b1], axis=cb), ca, cb)
+
+    return stacked(ah, bl, al, bh) + stacked(ah, bm, am, bm) + stacked(ah, bh, am, bh)
 
 
 def tree_sum(terms):
@@ -82,16 +96,17 @@
         scaled.append(jnp.where(lane < k + 8, x, 0.0))
         if k + 8 < n:
             xs = [down(x, j) for j in range(8)]
+        copies = [[along(rows[g], k + j) for g in range(g0 + 1, n // 8)] for j in range(8)]
         for g in range(g0 + 1, n // 8):
-            rows[g] = jnp.where(own, 0.0, rows[g]) - tree_sum([along(rows[g], k + j) * xs[j] for j in range(8)])
-    return exact(jnp.concatenate(unit, axis=0), jnp.concatenate(scaled, axis=0), 0, 0)
+            rows[g] = jnp.where(own, 0.0, rows[g]) - tree_sum([copies[j][g - g0 - 1] * xs[j] for j in range(8)])
+    return exact(jnp.concatenate(unit, axis=0).T, jnp.concatenate(scaled, axis=0), 1, 0)
 
 
 def compaction_kernel(
     qpos_hbm, q_hbm, k_hbm, v_hbm, slots_hbm,
     own_out, fitted_ref,
     qpos_ref, q_ref, k_ref, v_ref, slots_ref,
-    q_1, q_2, qp_1, qp_2, c_0, c_1, c_2, c_3, vt, n_0, n_1, s_1, n_2, s_2, o_3, feats,
+    q_1, q_2, qp_1, qp_2, c_0, c_1, c_2, c_3, vt, n_0, n_1, s_1, n_2, s_2, o_3, feats, gram, inverse, lower, upper, share, rest,
     load_sems, send_sems, recv_sems,
 ):
     me = lax.axis_index("pos")
@@ -119,20 +134,36 @@
     for load in loads[:4]:
         load.wait()
 
-    started = []
-
-    def send(stream, axis, o, src, dst):
-        copy = pltpu.make_async_remote_copy(
-            src_ref=src, dst_ref=dst, send_sem=send_sems.at[stream, o], recv_sem=recv_sems.at[stream, o],
+    def copy_of(stream, axis, o, src, dst):
+        return pltpu.make_async_remote_copy(
+            src_ref=src, dst_ref=dst, send_sem=send_sems.at[stream], recv_sem=recv_sems.at[stream],
             device_id=peer(axis, o), device_id_type=MESH_ID,
         )
-        copy.start()
-        started.append(copy)
-        return copy
-
-    def arrive(copies):
-        for copy in copies:
-            copy.wait_recv()
+
+    def all_of(stream, buffer):
+        seven = buffer.at[pl.ds(0, RING - 1)]
+        return copy_of(stream, 0, 1, seven, seven)
+
+    def send_all(*streams):
+        for o in offsets:
+            for stream, axis, src_of, dst_of, _ in streams:
+                copy_of(stream, axis, o, src_of(o), dst_of(o)).start()
+        return [(stream, buffer) for stream, _, _, _, buffer in streams]
+
+    def gather(stream, axis, buffer, slot):
+        return (stream, axis, lambda o: buffer.at[slot], lambda o: buffer.at[slot], buffer)
+
+    def spread(stream, axis, buffer):
+        return (stream, axis, lambda o: buffer.at[0], lambda o: buffer.at[o], buffer)
+
+    def scatter(stream, axis, source, buffer):
+        return (
+            stream, axis, lambda o: source.at[lax.rem(place[axis] + o, RING)], lambda o: buffer.at[o], buffer
+        )
+
+    def arrive(streams):
+        for stream, buffer in streams:
+            all_of(stream, buffer).wait_recv()
 
     halves = (0, 1)
 
@@ -159,24 +190,24 @@
 
     pl.semaphore_wait(barrier, 2 * (RING - 1))
 
-    get_q = [send(h, 1 - h, o, q_1.at[h, place[1 - h]], q_1.at[h, place[1 - h]]) for h in halves for o in offsets]
-    get_qp = [send(2, 1, o, qp_1.at[0], qp_1.at[o]) for o in offsets]
-    get_c = [send(3 + h, h, o, c_0.at[h, lax.rem(place[h] + o, RING)], c_1.at[h, o]) for o in offsets for h in halves]
+    get_q = send_all(*(gather(h, 1 - h, q_1.at[h], place[1 - h]) for h in halves))
+    get_qp = send_all(spread(2, 1, qp_1))
+    get_c = send_all(*(scatter(3 + h, h, c_0.at[h], c_1.at[h]) for h in halves))
     loads[4].wait()
     vt[...] = v_ref[...].astype(F32).T.astype(BF16)
 
     arrive(get_q)
     for h in halves:
         q_2[h, place[h]] = q_1[h].reshape(RING * QROWS, DH).astype(BF16)
-    get_q = [send(5 + h, h, o, q_2.at[h, place[h]], q_2.at[h, place[h]]) for o in offsets for h in halves]
+    get_q = send_all(*(gather(5 + h, h, q_2.at[h], place[h]) for h in halves))
     arrive(get_qp)
     qp_2[0] = tree_sum([qp_1[o] for o in range(RING)])
-    get_qp = [send(7, 0, o, qp_2.at[0], qp_2.at[o]) for o in offsets]
+    get_qp = send_all(spread(7, 0, qp_2))
 
     arrive(get_c)
     for h in halves:
         c_2[h, 0] = tree_sum([c_0[h, place[h]].astype(F32)] + [c_1[h, o].astype(F32) for o in offsets]).astype(BF16)
-    get_c = [send(8 + h, 1 - h, o, c_2.at[h, 0], c_2.at[h, o]) for o in offsets for h in halves]
+    get_c = send_all(*(spread(8 + h, 1 - h, c_2.at[h]) for h in halves))
 
     arrive(get_q)
     arrive(get_qp)
@@ -186,10 +217,9 @@
     arrive(get_c)
     for h in halves:
         c_3[h, place[h]] = tree_sum([c_2[h, o].astype(F32) for o in range(RING)]).astype(BF16)
-    get_c = [send(10 + h, h, o, c_3.at[h, place[h]], c_3.at[h, place[h]]) for o in offsets for h in halves]
+    get_c = send_all(*(gather(10 + h, h, c_3.at[h], place[h]) for h in halves))
 
     key_pos = lax.broadcasted_iota(jnp.int32, (BLOCK, LANES), 0) + base
-    get_s, get_n = [], []
     for h in halves:
         tops, totals = [], []
         for c in (0, 1):
@@ -202,10 +232,9 @@
             totals.append(jnp.sum(weights, axis=0, keepdims=True))
             n_0[h, :, :, chunk(c)] = dot(vt[...], weights.astype(BF16), 1, 0).reshape(RING, SLAB, LANES)
         s_1[h, 0] = jnp.concatenate(tops + totals, axis=0)
-    for o in offsets:
-        for h in halves:
-            get_s.append(send(12 + h, h, o, s_1.at[h, 0], s_1.at[h, o]))
-            get_n.append(send(14 + h, h, o, n_0.at[h, lax.rem(place[h] + o, RING)], n_1.at[h, o]))
+    get_n = send_all(
+        *(spread(12 + h, h, s_1.at[h]) for h in halves), *(scatter(14 + h, h, n_0.at[h], n_1.at[h]) for h in halves)
+    )
 
     def merge(stats, first, others, c):
         top = stats[0][c:c + 1]
@@ -231,7 +260,6 @@
         raw = jnp.where(allowed, jnp.exp(masked - top), 0.0)
         feats[:, chunk(c)] = (raw * (1.0 / jnp.sum(raw, axis=0, keepdims=True))).astype(BF16)
     diagonal = lax.broadcasted_iota(jnp.int32, (LANES, LANES), 0) == lax.broadcasted_iota(jnp.int32, (LANES, LANES), 1)
-    gram = {}
     for i in range(CHUNKS):
         for j in range(i + 1):
             block = dot(feats[chunk(i), :], feats[chunk(j), :], 1, 1)
@@ -243,9 +271,8 @@
             s_2[h, 0] = jnp.concatenate([m[0] for m in merged] + [m[1] for m in merged], axis=0)
             for c in (0, 1):
                 n_2[h, 0, :, chunk(c)] = merged[c][2]
-        return (
-            [send(16 + h, 1 - h, o, s_2.at[h, 0], s_2.at[h, o]) for o in offsets for h in halves]
-            + [send(18 + h, 1 - h, o, n_2.at[h, 0], n_2.at[h, o]) for o in offsets for h in halves]
+        send_all(
+            *(spread(16 + h, 1 - h, s_2.at[h]) for h in halves), *(spread(18 + h, 1 - h, n_2.at[h]) for h in halves)
         )
 
     def merge_second():
@@ -253,67 +280,70 @@
             for c in (0, 1):
                 _, total, numer = merge([s_2[h, o] for o in range(RING)], n_2[h, 0], n_2[h], c)
                 o_3[h, place[h], :, chunk(c)] = (numer / total).astype(BF16)
-        return [send(20 + h, h, o, o_3.at[h, place[h]], o_3.at[h, place[h]]) for o in offsets for h in halves]
-
-    inverse, lower, upper = {}, {}, {}
-
-    def update(i, j, c):
-        gram[i, j] = gram[i, j] - exact(lower[i, c], gram[j, c], 1, 1)
-
-    def step(c):
-        inverse[c] = invert_spd(gram[c, c])
-        if c + 1 < CHUNKS:
-            lower[c + 1, c] = exact(gram[c + 1, c], inverse[c], 1, 0)
-            update(c + 1, c + 1, c)
-
-    def rest(c):
-        for i in range(c + 2, CHUNKS):
-            lower[i, c] = exact(gram[i, c], inverse[c], 1, 0)
-            for j in range(c + 1, i + 1):
-                update(i, j, c)
-        for i in range(c + 1, CHUNKS):
-            upper[c, i] = exact(inverse[c], gram[i, c], 1, 1)
-
-    arrive(get_s)
+        send_all(*(gather(20 + h, h, o_3.at[h], place[h]) for h in halves))
+
     arrive(get_n)
-    get_n = merge_first()
-    step(0)
-    arrive(get_n)
-    get_o = merge_second()
-    rest(0)
-    step(1)
-    rest(1)
-    step(2)
-    arrive(get_o)
-    attended = jnp.concatenate([o_3[h].reshape(DH, HALF) for h in halves], axis=1)
-    row = lax.broadcasted_iota(jnp.int32, (RING, BLOCK), 0)
-    column = lax.broadcasted_iota(jnp.int32, (RING, BLOCK), 1)
-    pick = jnp.zeros((RING, BLOCK), F32)
-    for i in range(RING):
-        pick = jnp.where((row == i) & (column == own_id[i]), 1.0, pick)
-    own_out[...] = dot(pick.astype(BF16), attended, 1, 1).astype(BF16)
-    rest(2)
-    part = [dot(feats[chunk(i), :], attended, 1, 1) for i in range(CHUNKS)]
-    for c in range(CHUNKS - 1):
-        for i in range(c + 1, CHUNKS):
-            part[i] = part[i] - exact(lower[i, c], part[c], 1, 0)
+    merge_first()
     last = CHUNKS - 1
-    share = {}
-    for c in reversed(range(last)):
-        part[c] = exact(inverse[c], part[c], 1, 0)
-        share[c] = -upper[c, last]
-        for i in range(c + 1, last):
-            part[c] = part[c] - exact(upper[c, i], part[i], 1, 0)
-            share[c] = share[c] - exact(upper[c, i], share[i], 1, 0)
-    step(last)
-    part[last] = exact(inverse[last], part[last], 1, 0)
-    fitted_ref[chunk(last), :] = part[last]
-    for c in range(last):
-        fitted_ref[chunk(c), :] = part[c] + exact(share[c], part[last], 1, 0)
-    for copy in started:
-        copy.wait_send()
-
-
+
+    def after(c):
+        if c < last:
+            for i in range(c + 1, CHUNKS):
+                lower[i, c] = exact(gram[i, c], inverse[c], 1, 0)
+                upper[c, i] = exact(inverse[c], gram[i, c], 1, 1)
+            for i in range(c + 1, CHUNKS):
+                for j in range(c + 1, i + 1):
+                    gram[i, j] = gram[i, j] - exact(lower[i, c], gram[j, c], 1, 1)
+        if c == MERGE_AFTER:
+            arrive([(16 + h, s_2.at[h]) for h in halves] + [(18 + h, n_2.at[h]) for h in halves])
+            merge_second()
+        if c == last - 1:
+            arrive([(20 + h, o_3.at[h]) for h in halves])
+            attended = jnp.concatenate([o_3[h].reshape(DH, HALF) for h in halves], axis=1)
+            row = lax.broadcasted_iota(jnp.int32, (RING, BLOCK), 0)
+            column = lax.broadcasted_iota(jnp.int32, (RING, BLOCK), 1)
+            pick = jnp.zeros((RING, BLOCK), F32)
+            for i in range(RING):
+                pick = jnp.where((row == i) & (column == own_id[i]), 1.0, pick)
+            own_out[...] = dot(pick.astype(BF16), attended, 1, 1).astype(BF16)
+            part = [dot(feats[chunk(i), :], attended, 1, 1) for i in range(CHUNKS)]
+            for c in range(last):
+                for i in range(c + 1, CHUNKS):
+                    part[i] = part[i] - exact(lower[i, c], part[c], 1, 0)
+            rest[...] = part[last]
+            for c in reversed(range(last)):
+                part[c] = exact(inverse[c], part[c], 1, 0)
+                shared = -upper[c, last]
+                for i in range(c + 1, last):
+                    part[c] = part[c] - exact(upper[c, i], part[i], 1, 0)
+                    shared = shared - exact(upper[c, i], share[i], 1, 0)
+                share[c] = shared
+                fitted_ref[chunk(c), :] = part[c]
+            everything = [(2, qp_1), (7, qp_2)] + [
+                (stream + h, buffer.at[h])
+                for stream, buffer in [
+                    (0, q_1), (3, c_1), (5, q_2), (8, c_2), (10, c_3), (12, s_1), (14, n_1), (16, s_2), (18, n_2), (20, o_3)
+                ]
+                for h in halves
+            ]
+            for stream, buffer in everything:
+                all_of(stream, buffer).wait_send()
+        if c == last:
+            solved = exact(inverse[last], rest[...], 1, 0)
+            fitted_ref[chunk(last), :] = solved
+            for i in range(last):
+                fitted_ref[chunk(i), :] = fitted_ref[chunk(i), :] + exact(share[i], solved, 1, 0)
+
+    def eliminate(b, carry):
+        inverse[b] = invert_spd(gram[b, b])
+        for c in range(CHUNKS):
+            pl.when(b == c)(functools.partial(after, c))
+        return carry
+
+    lax.fori_loop(0, CHUNKS, eliminate, 0)
+
+
+MERGE_AFTER = 0
 STREAMS = 22
 
 
@@ -321,6 +351,7 @@
     vmem = pl.BlockSpec(memory_space=pltpu.VMEM)
     table = pltpu.VMEM((2, RING, SLAB, HALF), BF16)
     wide = pltpu.VMEM((2, RING, SLAB, HALF), F32)
+    blocks = pltpu.VMEM((CHUNKS, CHUNKS, LANES, LANES), F32)
     stats = pltpu.VMEM((2, RING, CHUNKS, LANES), F32)
     return pl.pallas_call(
         compaction_kernel,
@@ -344,9 +375,14 @@
             pltpu.VMEM((DH, BLOCK), BF16),
             wide, wide, stats, wide, stats, table,
             pltpu.VMEM((BLOCK, BLOCK), BF16),
+            blocks,
+            pltpu.VMEM((CHUNKS, LANES, LANES), F32),
+            blocks, blocks,
+            pltpu.VMEM((CHUNKS, LANES, LANES), F32),
+            pltpu.VMEM((LANES, DH), F32),
             pltpu.SemaphoreType.DMA((5,)),
-            pltpu.SemaphoreType.DMA((STREAMS, RING)),
-            pltpu.SemaphoreType.DMA((STREAMS, RING)),
+            pltpu.SemaphoreType.DMA((STREAMS,)),
+            pltpu.SemaphoreType.DMA((STREAMS,)),
         ],
         compiler_params=pltpu.CompilerParams(collective_id=0, has_side_effects=True, vmem_limit_bytes=VMEM_LIMIT),
         name="compaction",

time: 61.9 us -> 51.9 us (0.84)
  Pallas kernels: 59.9 us -> 49.8 us
    pallas_call x1, Pallas kernels: 59.9 us -> 49.8 us  [compaction(): pl.pallas_call(compaction_kernel, out_shape=(jax.ShapeDtypeStruct((RING,...]
where the time goes in v4:
time: 51.9 us; the launch traced here: 51.8 us
  Pallas kernels  49.8 us (96%)
  local copies, waits for them, and re-layouts  1.28 us (2%)
  between operations  0.64 us (1%)
    pallas_call x1, Pallas kernels, compaction(): pl.pallas_call(compaction_kernel, out_shape=(jax.ShapeDtypeStruct((RING,...  49.8 us
    unnamed x2, local copies, waits for them, and re-layouts  1.28 us

profile of v4, /device:TPU:6, one launch (start us, length us, event | category | flops | bytes accessed | tf_op | source)
XLA Modules:
  0.0 51.8 jit_solution(3197488922924503275)
XLA Ops:
  0.6 49.8 %compaction.1 = (bf16[8,128]{1,0:T(8,128)(2,1)S(1)}, f32[512,128]{1,0:T(8,128)S(1)}) custom-call(s32[1,8]{1,0:T(1,128)} %qpos_hbm.1, bf16[8,128]{1,0:T(8,128)(2,1)} %bitcast.9, bf16[512,128]{1,0:T(8,128)(2,1)} %bitcast.7, bf16[512,128]{1,0:T(8,128)(2,1)} %bitcast.8, s32[1,512]{1,0:T(1,128)} %slots_hbm.1), custom_call_target="tpu_custom_call" | custom-call | tf_op jit(solution)/shard_map/compaction/pallas_call | solution.py:356
  50.5 0.6 %copy.9 = bf16[1,8,128]{2,1,0:T(8,128)(2,1)} copy(bf16[1,8,128]{2,1,0:T(8,128)(2,1)S(1)} %bitcast.6) | data formatting | bytes 4096
  51.1 0.7 %copy.10 = f32[1,512,128]{2,1,0:T(8,128)} copy(f32[1,512,128]{2,1,0:T(8,128)S(1)} %bitcast.5) | data formatting | bytes 524288

commit v5 on v4

--- a/solution.py
+++ b/solution.py
@@ -39,14 +39,23 @@
     return high, middle, (rest - middle.astype(F32)).astype(BF16)
 
 
+def stacked(ca, cb, *pairs):
+    return dot(
+        jnp.concatenate([a for a, _ in pairs], axis=ca), jnp.concatenate([b for _, b in pairs], axis=cb), ca, cb
+    )
+
+
 def exact(a, b, ca, cb):
     ah, am, al = pieces(a)
     bh, bm, bl = pieces(b)
-
-    def stacked(a0, b0, a1, b1):
-        return dot(jnp.concatenate([a0, a1], axis=ca), jnp.concatenate([b0, b1], axis=cb), ca, cb)
-
-    return stacked(ah, bl, al, bh) + stacked(ah, bm, am, bm) + stacked(ah, bh, am, bh)
+    small = stacked(ca, cb, (ah, bl), (al, bh))
+    return small + stacked(ca, cb, (ah, bm), (am, bm)) + stacked(ca, cb, (ah, bh), (am, bh))
+
+
+def close(pairs):
+    split = [(pieces(a), pieces(b)) for a, b in pairs]
+    cross_terms = [term for (ah, am, _), (bh, bm, _) in split for term in ((ah, bm), (am, bh))]
+    return stacked(1, 0, *cross_terms) + stacked(1, 0, *[(a[0], b[0]) for a, b in split])
 
 
 def tree_sum(terms):
@@ -66,11 +75,10 @@
     def down(v, i):
         return jnp.broadcast_to(v[i:i + 1, :], (8, n))
 
-    rows = [a[8 * g:8 * g + 8, :] for g in range(n // 8)]
-    unit, scaled = [], []
-    for g0 in range(n // 8):
-        k = 8 * g0
-        m = [jnp.where(lane < n + j, along(rows[g0], k + j), 0.0) for j in range(8)]
+    def kept(v):
+        return [jnp.where(lane < n + j, u, 0.0) for j, u in enumerate(v)]
+
+    def invert_pivot(m):
         for t in range(0, 8, 2):
             p00, p10, p11 = down(m[t], t), down(m[t], t + 1), down(m[t + 1], t + 1)
             scale = 1.0 / (p00 * p11 - p10 * p10)
@@ -89,16 +97,51 @@
                     x0, x1 = i00 * w0 + i10 * w1, i10 * w0 + i11 * w1
                     new.append(jnp.where(pivots, 0.0, m[j]) - (f0 * x0 + f1 * x1))
             m = new
-        own = (lane >= k) & (lane < k + 8)
-        w = jnp.where(own, jnp.where(lane - k == sub, 1.0, 0.0), rows[g0])
-        x = tree_sum([m[j] * down(w, j) for j in range(8)])
+        return m
+
+    rows = [a[8 * g:8 * g + 8, :] for g in range(n // 8)]
+    middle = n // 16
+    unit, scaled, unit_half, scaled_half = [], [], [], []
+
+    def solve_row(g, inverted):
+        k = 8 * g
+        w = jnp.where((lane >= k) & (lane < k + 8), jnp.where(lane - k == sub, 1.0, 0.0), rows[g])
+        x = tree_sum([inverted[j] * down(w, j) for j in range(8)])
         unit.append(jnp.where(lane < k + 8, w, 0.0))
         scaled.append(jnp.where(lane < k + 8, x, 0.0))
-        if k + 8 < n:
-            xs = [down(x, j) for j in range(8)]
-        copies = [[along(rows[g], k + j) for g in range(g0 + 1, n // 8)] for j in range(8)]
-        for g in range(g0 + 1, n // 8):
-            rows[g] = jnp.where(own, 0.0, rows[g]) - tree_sum([copies[j][g - g0 - 1] * xs[j] for j in range(8)])
+        if g < middle:
+            unit_half.append(w)
+            scaled_half.append(jnp.where((lane < k + 8) | (lane >= n // 2), x, 0.0))
+        return [down(x, j) for j in range(8)]
+
+    def eliminate_row(g, of, factors, xs):
+        k = 8 * of
+        own = (lane >= k) & (lane < k + 8)
+        rows[g] = jnp.where(own, 0.0, rows[g]) - tree_sum([factors[j] * xs[j] for j in range(8)])
+
+    for g0 in range(0, n // 8, 2):
+        if g0 == middle:
+            share = exact(jnp.concatenate(unit_half, axis=0).T[n // 2:, :], jnp.concatenate(scaled_half, axis=0), 1, 0)
+            for g in range(middle, n // 8):
+                rows[g] = jnp.where(lane < n // 2, 0.0, rows[g]) - share[8 * (g - middle):8 * (g - middle) + 8, :]
+        g1 = g0 + 1
+        m = kept([along(rows[g0], 8 * g0 + j) for j in range(8)])
+        b = kept([along(rows[g1], 8 * g0 + j) for j in range(8)])
+        m1 = [along(rows[g1], 8 * g1 + j) for j in range(8)]
+        later = range(g0 + 2, middle if g0 < middle else n // 8)
+        factors = {g: [along(rows[g], 8 * g0 + j) for j in range(8)] for g in later}
+        m = invert_pivot(m)
+        bm = [tree_sum([b[i] * down(m[j], i) for i in range(8)]) for j in range(8)]
+        m1 = [m1[j] - tree_sum([bm[i] * down(b[i], j) for i in range(8)]) for j in range(8)]
+        xs = solve_row(g0, m)
+        eliminate_row(g1, g0, b, xs)
+        for g in later:
+            eliminate_row(g, g0, factors[g], xs)
+        factors = {g: [along(rows[g], 8 * g1 + j) for j in range(8)] for g in later}
+        m1 = invert_pivot(m1)
+        xs = solve_row(g1, m1)
+        for g in later:
+            eliminate_row(g, g1, factors[g], xs)
     return exact(jnp.concatenate(unit, axis=0).T, jnp.concatenate(scaled, axis=0), 1, 0)
 
 
@@ -307,18 +350,15 @@
                 pick = jnp.where((row == i) & (column == own_id[i]), 1.0, pick)
             own_out[...] = dot(pick.astype(BF16), attended, 1, 1).astype(BF16)
             part = [dot(feats[chunk(i), :], attended, 1, 1) for i in range(CHUNKS)]
-            for c in range(last):
-                for i in range(c + 1, CHUNKS):
-                    part[i] = part[i] - exact(lower[i, c], part[c], 1, 0)
+            for i in range(1, CHUNKS):
+                part[i] = part[i] - close([(lower[i, j], part[j]) for j in range(i)])
             rest[...] = part[last]
-            for c in reversed(range(last)):
-                part[c] = exact(inverse[c], part[c], 1, 0)
-                shared = -upper[c, last]
-                for i in range(c + 1, last):
-                    part[c] = part[c] - exact(upper[c, i], part[i], 1, 0)
-                    shared = shared - exact(upper[c, i], share[i], 1, 0)
-                share[c] = shared
-                fitted_ref[chunk(c), :] = part[c]
+            for i in reversed(range(last)):
+                part[i] = jnp.concatenate([close([(inverse[i], part[i])]), -upper[i, last]], axis=1)
+                if i + 1 < last:
+                    part[i] = part[i] - close([(upper[i, j], part[j]) for j in range(i + 1, last)])
+                fitted_ref[chunk(i), :] = part[i][:, :DH]
+                share[i] = part[i][:, DH:]
             everything = [(2, qp_1), (7, qp_2)] + [
                 (stream + h, buffer.at[h])
                 for stream, buffer in [
@@ -329,10 +369,10 @@
             for stream, buffer in everything:
                 all_of(stream, buffer).wait_send()
         if c == last:
-            solved = exact(inverse[last], rest[...], 1, 0)
+            solved = close([(inverse[last], rest[...])])
             fitted_ref[chunk(last), :] = solved
             for i in range(last):
-                fitted_ref[chunk(i), :] = fitted_ref[chunk(i), :] + exact(share[i], solved, 1, 0)
+                fitted_ref[chunk(i), :] = fitted_ref[chunk(i), :] + close([(share[i], solved)])
 
     def eliminate(b, carry):
         inverse[b] = invert_spd(gram[b, b])
@@ -392,12 +432,32 @@
 VMEM_LIMIT = 32 * 1024 * 1024
 
 
+def emit_kernel(own_ref, fitted_ref, own_out, fitted_out):
+    own_out[0] = own_ref[...]
+    fitted_out[0] = fitted_ref[...]
+
+
+def emit(own, fitted):
+    vmem = pl.BlockSpec(memory_space=pltpu.VMEM)
+    return pl.pallas_call(
+        emit_kernel,
+        out_shape=(
+            jax.ShapeDtypeStruct((1, RING, DH), BF16),
+            jax.ShapeDtypeStruct((1, BLOCK, DH), F32),
+        ),
+        in_specs=[vmem] * 2,
+        out_specs=(vmem,) * 2,
+        compiler_params=pltpu.CompilerParams(vmem_limit_bytes=VMEM_LIMIT),
+        name="emit",
+    )(own, fitted)
+
+
 def shards(ref_queries, query_pos, cache_keys, cache_values, slot_index):
     own, fitted = compaction(*(
         pltpu.with_memory_space_constraint(x, pltpu.HBM)
         for x in (ref_queries[0], query_pos, cache_keys[0], cache_values[0], slot_index)
     ))
-    return (own[None], fitted[None])
+    return emit(own, fitted)
 
 
 def solution(mesh):

time: 51.9 us -> 49.5 us (0.954)
  local copies, waits for them, and re-layouts: 1.28 us -> 0 us
  Pallas kernels: 49.8 us -> 48.7 us
    pallas_call x1, Pallas kernels: 49.8 us -> 48 us  [compaction(): pl.pallas_call(compaction_kernel, out_shape=(jax.ShapeDtypeStruct((RING,...]
    unnamed x2 -> x0, local copies, waits for them, and re-layouts: 1.28 us -> none
    pallas_call x0 -> x1, Pallas kernels: none -> 0.72 us  [emit(): pl.pallas_call(emit_kernel, out_shape=(jax.ShapeDtypeStruct((1, RING, DH)...]
where the time goes in v5:
time: 49.5 us; the launch traced here: 49.3 us
  Pallas kernels  48.7 us (98%)
  between operations  0.64 us (1%)
    pallas_call x1, Pallas kernels, compaction(): pl.pallas_call(compaction_kernel, out_shape=(jax.ShapeDtypeStruct((RING,...  48 us

profile of v5, /device:TPU:6, one launch (start us, length us, event | category | flops | bytes accessed | tf_op | source)
XLA Modules:
  0.0 49.3 jit_solution(17108411807341888715)
XLA Ops:
  0.6 48.0 %compaction.1 = (bf16[8,128]{1,0:T(8,128)(2,1)S(1)}, f32[512,128]{1,0:T(8,128)S(1)}) custom-call(s32[1,8]{1,0:T(1,128)} %qpos_hbm.1, bf16[8,128]{1,0:T(8,128)(2,1)} %bitcast.5, bf16[512,128]{1,0:T(8,128)(2,1)} %bitcast.3, bf16[512,128]{1,0:T(8,128)(2,1)} %bitcast.4, s32[1,512]{1,0:T(1,128)} %slots_hbm.1), custom_call_target="tpu_custom_call" | custom-call | tf_op jit(solution)/shard_map/compaction/pallas_call | solution.py:396
  48.6 0.7 %emit.1 = (bf16[1,8,128]{2,1,0:T(8,128)(2,1)}, f32[1,512,128]{2,1,0:T(8,128)}) custom-call(bf16[8,128]{1,0:T(8,128)(2,1)S(1)} %get-tuple-element.4.own_ref, f32[512,128]{1,0:T(8,128)S(1)} %get-tuple-element.5.fitted_ref), custom_call_target="tpu_custom_call" | custom-call | tf_op jit(solution)/shard_map/emit/pallas_call | solution.py:442

commit v6 on v5

--- a/solution.py
+++ b/solution.py
@@ -64,7 +64,7 @@
     return terms[0]
 
 
-def invert_spd(a):
+def factor_spd(a, halfway):
     n = a.shape[0]
     sub = lax.broadcasted_iota(jnp.int32, (8, n), 0)
     lane = lax.broadcasted_iota(jnp.int32, (8, n), 1)
@@ -121,6 +121,7 @@
 
     for g0 in range(0, n // 8, 2):
         if g0 == middle:
+            halfway()
             share = exact(jnp.concatenate(unit_half, axis=0).T[n // 2:, :], jnp.concatenate(scaled_half, axis=0), 1, 0)
             for g in range(middle, n // 8):
                 rows[g] = jnp.where(lane < n // 2, 0.0, rows[g]) - share[8 * (g - middle):8 * (g - middle) + 8, :]
@@ -142,14 +143,14 @@
         xs = solve_row(g1, m1)
         for g in later:
             eliminate_row(g, g1, factors[g], xs)
-    return exact(jnp.concatenate(unit, axis=0).T, jnp.concatenate(scaled, axis=0), 1, 0)
+    return jnp.concatenate(unit, axis=0).T, jnp.concatenate(scaled, axis=0)
 
 
 def compaction_kernel(
     qpos_hbm, q_hbm, k_hbm, v_hbm, slots_hbm,
     own_out, fitted_ref,
     qpos_ref, q_ref, k_ref, v_ref, slots_ref,
-    q_1, q_2, qp_1, qp_2, c_0, c_1, c_2, c_3, vt, n_0, n_1, s_1, n_2, s_2, o_3, feats, gram, inverse, lower, upper, share, rest,
+    q_1, q_2, qp_1, qp_2, c_0, c_1, c_2, c_3, vt, n_0, n_1, s_1, n_2, s_2, o_3, feats, gram, inverse, lower, upper, share, rest, unit, scaled,
     load_sems, send_sems, recv_sems,
 ):
     me = lax.axis_index("pos")
@@ -162,8 +163,8 @@
 
     offsets = (4, 3, 5, 2, 6, 1, 7)
     barrier = pltpu.get_barrier_semaphore()
-    for axis in (0, 1):
-        for o in offsets:
+    for o in offsets:
+        for axis in (0, 1):
             pl.semaphore_signal(barrier, inc=1, device_id=peer(axis, o), device_id_type=MESH_ID)
 
     loads = [
@@ -275,7 +276,7 @@
             totals.append(jnp.sum(weights, axis=0, keepdims=True))
             n_0[h, :, :, chunk(c)] = dot(vt[...], weights.astype(BF16), 1, 0).reshape(RING, SLAB, LANES)
         s_1[h, 0] = jnp.concatenate(tops + totals, axis=0)
-    get_n = send_all(
+    send_all(
         *(spread(12 + h, h, s_1.at[h]) for h in halves), *(scatter(14 + h, h, n_0.at[h], n_1.at[h]) for h in halves)
     )
 
@@ -309,6 +310,7 @@
             gram[i, j] = block + jnp.where(diagonal, RIDGE, 0.0) if i == j else block
 
     def merge_first():
+        arrive([(12 + h, s_1.at[h]) for h in halves] + [(14 + h, n_1.at[h]) for h in halves])
         for h in halves:
             merged = [merge([s_1[h, o] for o in range(RING)], n_0[h, place[h]], n_1[h], c) for c in (0, 1)]
             s_2[h, 0] = jnp.concatenate([m[0] for m in merged] + [m[1] for m in merged], axis=0)
@@ -325,21 +327,20 @@
                 o_3[h, place[h], :, chunk(c)] = (numer / total).astype(BF16)
         send_all(*(gather(20 + h, h, o_3.at[h], place[h]) for h in halves))
 
-    arrive(get_n)
-    merge_first()
     last = CHUNKS - 1
 
     def after(c):
+        if c == MERGE_AFTER:
+            arrive([(16 + h, s_2.at[h]) for h in halves] + [(18 + h, n_2.at[h]) for h in halves])
+            merge_second()
         if c < last:
+            inverse[c] = exact(unit[...], scaled[...], 1, 0)
             for i in range(c + 1, CHUNKS):
                 lower[i, c] = exact(gram[i, c], inverse[c], 1, 0)
                 upper[c, i] = exact(inverse[c], gram[i, c], 1, 1)
             for i in range(c + 1, CHUNKS):
                 for j in range(c + 1, i + 1):
                     gram[i, j] = gram[i, j] - exact(lower[i, c], gram[j, c], 1, 1)
-        if c == MERGE_AFTER:
-            arrive([(16 + h, s_2.at[h]) for h in halves] + [(18 + h, n_2.at[h]) for h in halves])
-            merge_second()
         if c == last - 1:
             arrive([(20 + h, o_3.at[h]) for h in halves])
             attended = jnp.concatenate([o_3[h].reshape(DH, HALF) for h in halves], axis=1)
@@ -369,13 +370,13 @@
             for stream, buffer in everything:
                 all_of(stream, buffer).wait_send()
         if c == last:
-            solved = close([(inverse[last], rest[...])])
+            solved = close([(unit[...], close([(scaled[...], rest[...])]))])
             fitted_ref[chunk(last), :] = solved
             for i in range(last):
                 fitted_ref[chunk(i), :] = fitted_ref[chunk(i), :] + close([(share[i], solved)])
 
     def eliminate(b, carry):
-        inverse[b] = invert_spd(gram[b, b])
+        unit[...], scaled[...] = factor_spd(gram[b, b], lambda: pl.when(b == 0)(merge_first))
         for c in range(CHUNKS):
             pl.when(b == c)(functools.partial(after, c))
         return carry
@@ -383,7 +384,7 @@
     lax.fori_loop(0, CHUNKS, eliminate, 0)
 
 
-MERGE_AFTER = 0
+MERGE_AFTER = 1
 STREAMS = 22
 
 
@@ -420,6 +421,8 @@
             blocks, blocks,
             pltpu.VMEM((CHUNKS, LANES, LANES), F32),
             pltpu.VMEM((LANES, DH), F32),
+            pltpu.VMEM((LANES, LANES), F32),
+            pltpu.VMEM((LANES, LANES), F32),
             pltpu.SemaphoreType.DMA((5,)),
             pltpu.SemaphoreType.DMA((STREAMS,)),
             pltpu.SemaphoreType.DMA((STREAMS,)),

time: 49.5 us -> 48.6 us (0.982)
  Pallas kernels: 48.7 us -> 47.8 us
    pallas_call x1, Pallas kernels: 48 us -> 47 us  [compaction(): pl.pallas_call(compaction_kernel, out_shape=(jax.ShapeDtypeStruct((RING,...]
where the time goes in v6:
time: 48.6 us; the launch traced here: 48.4 us
  Pallas kernels  47.8 us (98%)
  between operations  0.64 us (1%)
    pallas_call x1, Pallas kernels, compaction(): pl.pallas_call(compaction_kernel, out_shape=(jax.ShapeDtypeStruct((RING,...  47 us

profile of v6, /device:TPU:6, one launch (start us, length us, event | category | flops | bytes accessed | tf_op | source)
XLA Modules:
  0.0 48.4 jit_solution(386908854020096394)
XLA Ops:
  0.6 47.0 %compaction.1 = (bf16[8,128]{1,0:T(8,128)(2,1)S(1)}, f32[512,128]{1,0:T(8,128)S(1)}) custom-call(s32[1,8]{1,0:T(1,128)} %qpos_hbm.1, bf16[8,128]{1,0:T(8,128)(2,1)} %bitcast.5, bf16[512,128]{1,0:T(8,128)(2,1)} %bitcast.3, bf16[512,128]{1,0:T(8,128)(2,1)} %bitcast.4, s32[1,512]{1,0:T(1,128)} %slots_hbm.1), custom_call_target="tpu_custom_call" | custom-call | tf_op jit(solution)/shard_map/compaction/pallas_call | solution.py:397
  47.7 0.7 %emit.1 = (bf16[1,8,128]{2,1,0:T(8,128)(2,1)}, f32[1,512,128]{2,1,0:T(8,128)}) custom-call(bf16[8,128]{1,0:T(8,128)(2,1)S(1)} %get-tuple-element.4.own_ref, f32[512,128]{1,0:T(8,128)S(1)} %get-tuple-element.5.fitted_ref), custom_call_target="tpu_custom_call" | custom-call | tf_op jit(solution)/shard_map/emit/pallas_call | solution.py:445

commit v7 on v6

--- a/solution.py
+++ b/solution.py
@@ -150,7 +150,7 @@
     qpos_hbm, q_hbm, k_hbm, v_hbm, slots_hbm,
     own_out, fitted_ref,
     qpos_ref, q_ref, k_ref, v_ref, slots_ref,
-    q_1, q_2, qp_1, qp_2, c_0, c_1, c_2, c_3, vt, n_0, n_1, s_1, n_2, s_2, o_3, feats, gram, inverse, lower, upper, share, rest, unit, scaled,
+    q_1, q_2, qp_1, qp_2, c_0, c_1, c_2, c_3, vt, n_0, n_1, s_1, n_2, s_2, o_3, feats, gram, inverse, lower, upper, share, rest, unit, scaled, slot_col,
     load_sems, send_sems, recv_sems,
 ):
     me = lax.axis_index("pos")
@@ -208,6 +208,11 @@
     def arrive(streams):
         for stream, buffer in streams:
             all_of(stream, buffer).wait_recv()
+
+    def sent(tables):
+        for stream, buffer in tables:
+            for h in (0, 1):
+                all_of(stream + h, buffer.at[h]).wait_send()
 
     halves = (0, 1)
 
@@ -291,14 +296,16 @@
         )
         return top, total, numer
 
+    for c in range(CHUNKS):
+        slot_col[chunk(c), :] = jnp.broadcast_to(slots_ref[:, chunk(c)], (LANES, LANES)).T
+    all_of(2, qp_1).wait_send()
+    all_of(7, qp_2).wait_send()
+    sent([(0, q_1), (3, c_1), (5, q_2), (8, c_2)])
     arrive(get_c)
     compact = jnp.concatenate([c_3[h].reshape(DH, HALF).astype(F32).T for h in halves], axis=0).astype(BF16)
-    slot_col = jnp.concatenate(
-        [jnp.broadcast_to(slots_ref[:, chunk(c)], (LANES, LANES)).T for c in range(CHUNKS)], axis=0
-    )
     for c in range(CHUNKS):
         logits = dot(compact, queries[chunk(c), :], 1, 1) * INV_ROOT
-        allowed = slot_col <= qp[c:c + 1, :]
+        allowed = slot_col[...] <= qp[c:c + 1, :]
         masked = jnp.where(allowed, logits, NEG_FILL)
         top = jnp.max(masked, axis=0, keepdims=True)
         raw = jnp.where(allowed, jnp.exp(masked - top), 0.0)
@@ -337,11 +344,12 @@
             inverse[c] = exact(unit[...], scaled[...], 1, 0)
             for i in range(c + 1, CHUNKS):
                 lower[i, c] = exact(gram[i, c], inverse[c], 1, 0)
-                upper[c, i] = exact(inverse[c], gram[i, c], 1, 1)
+                upper[c, i] = lower[i, c].T
             for i in range(c + 1, CHUNKS):
                 for j in range(c + 1, i + 1):
                     gram[i, j] = gram[i, j] - exact(lower[i, c], gram[j, c], 1, 1)
         if c == last - 1:
+            sent([(10, c_3), (12, s_1), (14, n_1), (16, s_2), (18, n_2)])
             arrive([(20 + h, o_3.at[h]) for h in halves])
             attended = jnp.concatenate([o_3[h].reshape(DH, HALF) for h in halves], axis=1)
             row = lax.broadcasted_iota(jnp.int32, (RING, BLOCK), 0)
@@ -360,15 +368,7 @@
                     part[i] = part[i] - close([(upper[i, j], part[j]) for j in range(i + 1, last)])
                 fitted_ref[chunk(i), :] = part[i][:, :DH]
                 share[i] = part[i][:, DH:]
-            everything = [(2, qp_1), (7, qp_2)] + [
-                (stream + h, buffer.at[h])
-                for stream, buffer in [
-                    (0, q_1), (3, c_1), (5, q_2), (8, c_2), (10, c_3), (12, s_1), (14, n_1), (16, s_2), (18, n_2), (20, o_3)
-                ]
-                for h in halves
-            ]
-            for stream, buffer in everything:
-                all_of(stream, buffer).wait_send()
+            sent([(20, o_3)])
         if c == last:
             solved = close([(unit[...], close([(scaled[...], rest[...])]))])
             fitted_ref[chunk(last), :] = solved
@@ -423,6 +423,7 @@
             pltpu.VMEM((LANES, DH), F32),
             pltpu.VMEM((LANES, LANES), F32),
             pltpu.VMEM((LANES, LANES), F32),
+            pltpu.VMEM((BLOCK, LANES), jnp.int32),
             pltpu.SemaphoreType.DMA((5,)),
             pltpu.SemaphoreType.DMA((STREAMS,)),
             pltpu.SemaphoreType.DMA((STREAMS,)),

time: 48.6 us -> 48.4 us (level)
  no operation moved by 1% of the time
where the time goes in v7:
time: 48.4 us; the launch traced here: 48.2 us
  Pallas kernels  47.6 us (98%)
  between operations  0.64 us (1%)
    pallas_call x1, Pallas kernels, compaction(): pl.pallas_call(compaction_kernel, out_shape=(jax.ShapeDtypeStruct((RING,...  46.9 us

profile of v7, /device:TPU:6, one launch (start us, length us, event | category | flops | bytes accessed | tf_op | source)
XLA Modules:
  0.0 48.2 jit_solution(16548269949282902046)
XLA Ops:
  0.6 46.9 %compaction.1 = (bf16[8,128]{1,0:T(8,128)(2,1)S(1)}, f32[512,128]{1,0:T(8,128)S(1)}) custom-call(s32[1,8]{1,0:T(1,128)} %qpos_hbm.1, bf16[8,128]{1,0:T(8,128)(2,1)} %bitcast.5, bf16[512,128]{1,0:T(8,128)(2,1)} %bitcast.3, bf16[512,128]{1,0:T(8,128)(2,1)} %bitcast.4, s32[1,512]{1,0:T(1,128)} %slots_hbm.1), custom_call_target="tpu_custom_call" | custom-call | tf_op jit(solution)/shard_map/compaction/pallas_call | solution.py:397
  47.5 0.7 %emit.1 = (bf16[1,8,128]{2,1,0:T(8,128)(2,1)}, f32[1,512,128]{2,1,0:T(8,128)}) custom-call(bf16[8,128]{1,0:T(8,128)(2,1)S(1)} %get-tuple-element.4.own_ref, f32[512,128]{1,0:T(8,128)S(1)} %get-tuple-element.5.fitted_ref), custom_call_target="tpu_custom_call" | custom-call | tf_op jit(solution)/shard_map/emit/pallas_call | solution.py:446

commit v8 on v7

--- a/solution.py
+++ b/solution.py
@@ -328,6 +328,7 @@
         )
 
     def merge_second():
+        arrive([(16 + h, s_2.at[h]) for h in halves] + [(18 + h, n_2.at[h]) for h in halves])
         for h in halves:
             for c in (0, 1):
                 _, total, numer = merge([s_2[h, o] for o in range(RING)], n_2[h, 0], n_2[h], c)
@@ -337,9 +338,6 @@
     last = CHUNKS - 1
 
     def after(c):
-        if c == MERGE_AFTER:
-            arrive([(16 + h, s_2.at[h]) for h in halves] + [(18 + h, n_2.at[h]) for h in halves])
-            merge_second()
         if c < last:
             inverse[c] = exact(unit[...], scaled[...], 1, 0)
             for i in range(c + 1, CHUNKS):
@@ -376,7 +374,11 @@
                 fitted_ref[chunk(i), :] = fitted_ref[chunk(i), :] + close([(share[i], solved)])
 
     def eliminate(b, carry):
-        unit[...], scaled[...] = factor_spd(gram[b, b], lambda: pl.when(b == 0)(merge_first))
+        def halfway():
+            pl.when(b == 0)(merge_first)
+            pl.when(b == 1)(merge_second)
+
+        unit[...], scaled[...] = factor_spd(gram[b, b], halfway)
         for c in range(CHUNKS):
             pl.when(b == c)(functools.partial(after, c))
         return carry
@@ -384,7 +386,6 @@
     lax.fori_loop(0, CHUNKS, eliminate, 0)
 
 
-MERGE_AFTER = 1
 STREAMS = 22
 
 

time: 48.4 us -> 49.5 us (1.023)
  Pallas kernels: 47.6 us -> 48.7 us
    pallas_call x1, Pallas kernels: 46.9 us -> 48 us  [compaction(): pl.pallas_call(compaction_kernel, out_shape=(jax.ShapeDtypeStruct((RING,...]
where the time goes in v8:
time: 49.5 us; the launch traced here: 49.4 us
  Pallas kernels  48.7 us (98%)
  between operations  0.64 us (1%)
    pallas_call x1, Pallas kernels, compaction(): pl.pallas_call(compaction_kernel, out_shape=(jax.ShapeDtypeStruct((RING,...  48 us

profile of v8, /device:TPU:6, one launch (start us, length us, event | category | flops | bytes accessed | tf_op | source)
XLA Modules:
  0.0 49.4 jit_solution(2808809300476607184)
XLA Ops:
  0.6 48.0 %compaction.1 = (bf16[8,128]{1,0:T(8,128)(2,1)S(1)}, f32[512,128]{1,0:T(8,128)S(1)}) custom-call(s32[1,8]{1,0:T(1,128)} %qpos_hbm.1, bf16[8,128]{1,0:T(8,128)(2,1)} %bitcast.5, bf16[512,128]{1,0:T(8,128)(2,1)} %bitcast.3, bf16[512,128]{1,0:T(8,128)(2,1)} %bitcast.4, s32[1,512]{1,0:T(1,128)} %slots_hbm.1), custom_call_target="tpu_custom_call" | custom-call | tf_op jit(solution)/shard_map/compaction/pallas_call | solution.py:398
  48.6 0.7 %emit.1 = (bf16[1,8,128]{2,1,0:T(8,128)(2,1)}, f32[1,512,128]{2,1,0:T(8,128)}) custom-call(bf16[8,128]{1,0:T(8,128)(2,1)S(1)} %get-tuple-element.4.own_ref, f32[512,128]{1,0:T(8,128)S(1)} %get-tuple-element.5.fitted_ref), custom_call_target="tpu_custom_call" | custom-call | tf_op jit(solution)/shard_map/emit/pallas_call | solution.py:447
